TPU v7x, 128 devices: a whole 4x4x4 slice. The times are simulated.
128 devices in a mesh: ctx: 16 (over y, x), tp: 8 (over z, core).
Axes of the slice: x: 4, y: 4, z: 4, core: 2. Of those that a mesh axis runs over, the one named last changes fastest.
Arguments:
- qkv_first: bfloat16 [3, 16384, 4096], P(None, 'ctx', 'tp'), may hold values from -6 to 6
- short_first: float32 [3, 3, 4096], P(None, None, 'tp'), may hold values from -4 to 4
- medium_filter: bfloat16 [4096, 128], P('tp'), may hold values from -0.5 to 0.5
- out_weight: bfloat16 [4096, 4096], P('tp', 'ctx'), may hold values from -0.09375 to 0.09375
- residual_in: bfloat16 [16384, 4096], P('ctx', 'tp'), may hold values from -64 to 64
- norm_gain: bfloat16 [4096], P('tp'), may hold values from 0.5 to 1.5
- in_weight: bfloat16 [3, 4096, 4096], P(None, 'ctx', 'tp'), may hold values from -0.09375 to 0.09375
- short_second: float32 [3, 3, 4096], P(None, None, 'tp'), may hold values from -4 to 4
- rates: float32 [16, 4096], P(None, 'tp'), as said below
- residues: float32 [16, 4096], P(None, 'tp'), may hold values from -0.024 to 0.024
- skip_gain: float32 [4096], P('tp'), may hold values from -4 to 4
Outputs:
- hidden: bfloat16 [16384, 4096], P('ctx', 'tp')
- mixed: bfloat16 [16384, 4096], P('ctx', 'tp')
Inputs may be any that keep to these rules, and one draw needn't show every extreme that they name: `rates`: each entry is a positive decay rate per token, between 1e-7 and 0.05.
All inputs are finite; a program needn't handle non-finite values.
Results may differ from a plain program's by a relative error of at most 0.025.
Values may be sent and summed in bfloat16 or wider, within the bound.
No kernel may reach another device: no remote copies, remote signals or barrier semaphores. Data moves between devices by JAX's collectives and lax.ppermute only.
A program may use at most 128 MiB of HBM per device.

v0:
```python
import functools


import jax
import jax.numpy as jnp
from jax import lax
from jax.experimental import pallas as pl
from jax.experimental.pallas import tpu as pltpu
from jax.sharding import PartitionSpec as P

HALO = 144


def conv_kernel(extra, prev_ref, cur_ref, taps_ref, filt_ref, gain_ref, out_ref, k_ref, v_ref, g_ref, d_ref, r_ref, y_ref):
    length = cur_ref.shape[1]
    lag = 4 * filt_ref.shape[1]
    block = length // 8
    keep = lag + 8
    for ref, m in ((k_ref, 1), (v_ref, 2)):
        ref[:keep, :] = prev_ref[m, prev_ref.shape[1] - keep :, :].astype(jnp.float32)
        ref[keep:, :] = cur_ref[m].astype(jnp.float32)

    def feature(ref, m, at, rows):
        return (
            taps_ref[m, 0:1, :] * ref[pl.ds(at, rows), :]
            + taps_ref[m, 1:2, :] * ref[pl.ds(at - 1, rows), :]
            + taps_ref[m, 2:3, :] * ref[pl.ds(at - 2, rows), :]
        )

    for r in range(0, lag + length, 128):
        gated = feature(k_ref, 1, r + 8, 128) * feature(v_ref, 2, r + 8, 128)
        g_ref[r : r + 128, :] = gated.astype(jnp.bfloat16).astype(jnp.float32)

    def spread(k):
        return g_ref[pl.ds(k, 8, stride=block), :]

    for n in range((block + lag) // 4):
        e = [spread(4 * n + q) for q in range(4)]
        for w, (first, second) in enumerate(((e[0], e[2]), (e[1], e[3]), (e[0] + e[1], e[2] + e[3]))):
            d_ref[3 * w, n] = first
            d_ref[3 * w + 1, n] = second
            d_ref[3 * w + 2, n] = first + second
    count = block // 4 + 1
    base = lag // 4 - 1

    def short(n, carry):
        acc = [None] * count
        for q in range(lag // 4):
            weight = jnp.broadcast_to(filt_ref[n, pl.ds(q, 1), :], (8, 128))
            for i in range(count):
                term = weight * d_ref[n, base + i - q]
                acc[i] = term if q == 0 else acc[i] + term
        for i in range(count):
            r_ref[n, i] = acc[i]
        return carry

    lax.fori_loop(0, 9, short, 0)

    def joined(w, i):
        if i % 2:
            return r_ref[3 * w, i // 2 + 1] + r_ref[3 * w + 1, i // 2]
        return r_ref[3 * w + 2, i // 2] - r_ref[3 * w, i // 2] - r_ref[3 * w + 1, i // 2]

    late = joined(1, 0)
    for i in range(block // 2):
        even, odd, both = (joined(w, i + 1) for w in range(3))
        y_ref[pl.ds(2 * i, 8, stride=block), :] = even + late
        y_ref[pl.ds(2 * i + 1, 8, stride=block), :] = both - even - odd
        late = odd
    k_ref[:keep, :] = prev_ref[0, prev_ref.shape[1] - keep :, :].astype(jnp.float32)
    k_ref[keep:, :] = cur_ref[0].astype(jnp.float32)
    for r in range(0, length, 128):
        query = feature(k_ref, 0, keep + r, 128)
        out_ref[r : r + 128, :] = (query * y_ref[r : r + 128, :]).astype(jnp.bfloat16)
    if extra:
        out_ref[length:, :] = jnp.broadcast_to(gain_ref[...], (extra, 128))


def medium(prev, prev_rows, prev_at, qkv, at, taps, filt, gain, extra):
    length, channels = ROWS, qkv.shape[2]
    lag = 4 * filt.shape[1]
    return pl.pallas_call(
        functools.partial(conv_kernel, extra),
        out_shape=jax.ShapeDtypeStruct((length + extra, channels), jnp.bfloat16),
        grid=(channels // 128,),
        in_specs=[
            pl.BlockSpec((3, prev_rows, 128), lambda g: (0, prev_at, g)),
            pl.BlockSpec((3, length, 128), lambda g: (0, at, g)),
            pl.BlockSpec((3, 3, 128), lambda g: (0, 0, g)),
            pl.BlockSpec((9, lag // 4, 128), lambda g: (0, 0, g)),
            pl.BlockSpec((1, 128), lambda g: (0, g)),
        ],
        out_specs=pl.BlockSpec((length + extra, 128), lambda g: (0, g)),
        scratch_shapes=[
            pltpu.VMEM((length + lag + 8, 128), jnp.float32),
            pltpu.VMEM((length + lag + 8, 128), jnp.float32),
            pltpu.VMEM((length + lag, 128), jnp.float32),
            pltpu.VMEM((9, (length // 8 + lag) // 4, 8, 128), jnp.float32),
            pltpu.VMEM((9, length // 32 + 1, 8, 128), jnp.float32),
            pltpu.VMEM((length, 128), jnp.float32),
        ],
        compiler_params=pltpu.CompilerParams(vmem_limit_bytes=16 << 20),
        name="medium",
    )(prev, qkv, taps, filt, gain.reshape(1, channels))


def split_taps(filters):
    f = filters.T.astype(jnp.float32).reshape(-1, 4, filters.shape[0])
    rows = []
    for first, second in ((f[:, 0], f[:, 2]), (f[:, 1], f[:, 3]), (f[:, 0] + f[:, 1], f[:, 2] + f[:, 3])):
        rows += [first, second, first + second]
    return jnp.stack(rows)


def featurize_into(edge_ref, lower_ref, upper_ref, at_upper, at_lower, taps_ref, m, x_ref):
    half = lower_ref.shape[1]
    x_ref[:8, :] = edge_ref[at_upper, edge_ref.shape[1] - 8 :, :].astype(jnp.float32)
    x_ref[8 : half + 8, :] = lower_ref[at_lower].astype(jnp.float32)
    x_ref[half + 8 :, :] = upper_ref[at_upper].astype(jnp.float32)

    def at(r, rows):
        return (
            taps_ref[m, 0:1, :] * x_ref[pl.ds(r + 8, rows), :]
            + taps_ref[m, 1:2, :] * x_ref[pl.ds(r + 7, rows), :]
            + taps_ref[m, 2:3, :] * x_ref[pl.ds(r + 6, rows), :]
        )

    return at


def scan_kernel(
    edge_ref, lower_ref, upper_ref, taps_ref, rates_ref, u_ref, starts_ref, end_ref, k_ref, v_ref, g_ref, p_ref
):
    poles = rates_ref.shape[0]
    length = 2 * lower_ref.shape[1]
    block = length // 8
    kf = featurize_into(edge_ref, lower_ref, upper_ref, 1, 0, taps_ref, 1, k_ref)
    vf = featurize_into(edge_ref, lower_ref, upper_ref, 2, 1, taps_ref, 2, v_ref)
    for r in range(0, length, 128):
        gated = (kf(r, 128) * vf(r, 128)).astype(jnp.bfloat16)
        g_ref[r : r + 128, :] = gated.astype(jnp.float32)
    for i in range(block):
        u_ref[i] = g_ref[pl.ds(i, 8, stride=block), :]
    pole = [jnp.broadcast_to(jnp.exp(-rates_ref[n : n + 1, :]), (8, 128)) for n in range(poles)]

    def advance(i, states):
        states = list(states)
        for s in range(4):
            u = u_ref[i * 4 + s]
            states = [p * a + u for p, a in zip(pole, states)]
        return tuple(states)

    zero = jnp.zeros((8, 128), jnp.float32)
    states = lax.fori_loop(0, block // 4, advance, (zero,) * poles)
    for n in range(poles):
        decay = jnp.exp(-rates_ref[n : n + 1, :] * block)
        p_ref[...] = states[n]
        run = jnp.zeros((1, 128), jnp.float32)
        for b in range(8):
            starts_ref[n, b : b + 1, :] = run
            run = decay * run + p_ref[b : b + 1, :]
        end_ref[n : n + 1, :] = run.astype(jnp.bfloat16)


def modal_scan(edge, lower, upper, taps, rates):
    half, channels = lower.shape[1:]
    length = 2 * half
    poles = rates.shape[0]
    line = lambda rows: pl.BlockSpec((rows, 128), lambda g: (0, g))
    cube = lambda rows: pl.BlockSpec((rows, 8, 128), lambda g: (0, 0, g))
    return pl.pallas_call(
        scan_kernel,
        out_shape=(
            jax.ShapeDtypeStruct((length // 8, 8, channels), jnp.float32),
            jax.ShapeDtypeStruct((poles, 8, channels), jnp.float32),
            jax.ShapeDtypeStruct((poles, channels), jnp.bfloat16),
        ),
        grid=(channels // 128,),
        in_specs=[
            pl.BlockSpec((3, 16, 128), lambda g: (0, 0, g)),
            pl.BlockSpec((2, half, 128), lambda g: (0, 0, g)),
            pl.BlockSpec((3, half, 128), lambda g: (0, 0, g)),
            pl.BlockSpec((3, 3, 128), lambda g: (0, 0, g)),
            line(poles),
        ],
        out_specs=(cube(length // 8), cube(poles), line(poles)),
        scratch_shapes=[
            pltpu.VMEM((length + 8, 128), jnp.float32),
            pltpu.VMEM((length + 8, 128), jnp.float32),
            pltpu.VMEM((length, 128), jnp.float32),
            pltpu.VMEM((8, 128), jnp.float32),
        ],
        compiler_params=pltpu.CompilerParams(vmem_limit_bytes=16 << 20),
        name="modal_scan",
    )(edge, lower, upper, taps, rates)


def finish_kernel(
    edge_ref, lower_ref, upper_ref, taps_ref, rates_ref, residues_ref, skip_ref, u_ref, starts_ref, enter_ref, out_ref, q_ref, y_ref
):
    poles = rates_ref.shape[0]
    length = 2 * lower_ref.shape[1]
    block = length // 8
    pole = [jnp.broadcast_to(jnp.exp(-rates_ref[n : n + 1, :]), (8, 128)) for n in range(poles)]
    weight = [jnp.broadcast_to(residues_ref[n : n + 1, :], (8, 128)) for n in range(poles)]
    skip = jnp.broadcast_to(skip_ref[...], (8, 128))
    place = lax.broadcasted_iota(jnp.int32, (8, 128), 0).astype(jnp.float32) * block
    states = tuple(
        starts_ref[n] + jnp.exp(-rates_ref[n : n + 1, :] * place) * enter_ref[n : n + 1, :]
        for n in range(poles)
    )

    def advance(j, states):
        for s in range(4):
            i = j * 4 + s
            u = u_ref[i]
            states = [p * a + u for p, a in zip(pole, states)]
            parts = [w * a for w, a in zip(weight, states)] + [skip * u]
            while len(parts) > 1:
                parts = [a + b for a, b in zip(parts[::2], parts[1::2])] + parts[len(parts) & ~1 :]
            y_ref[pl.ds(i, 8, stride=block), :] = parts[0]
        return tuple(states)

    lax.fori_loop(0, block // 4, advance, states)
    qf = featurize_into(edge_ref, lower_ref, upper_ref, 0, 0, taps_ref, 0, q_ref)
    for r in range(0, length, 128):
        out_ref[r : r + 128, :] = (qf(r, 128) * y_ref[r : r + 128, :]).astype(jnp.bfloat16)


def modal_finish(edge, lower, upper, taps, rates, residues, skip, u, starts, enter):
    half, channels = lower.shape[1:]
    length = 2 * half
    poles = rates.shape[0]
    line = lambda rows: pl.BlockSpec((rows, 128), lambda g: (0, g))
    cube = lambda rows: pl.BlockSpec((rows, 8, 128), lambda g: (0, 0, g))
    return pl.pallas_call(
        finish_kernel,
        out_shape=jax.ShapeDtypeStruct((length, channels), jnp.bfloat16),
        grid=(channels // 128,),
        in_specs=[
            pl.BlockSpec((1, 16, 128), lambda g: (0, 0, g)),
            pl.BlockSpec((1, half, 128), lambda g: (0, 0, g)),
            pl.BlockSpec((1, half, 128), lambda g: (0, 0, g)),
            pl.BlockSpec((3, 3, 128), lambda g: (0, 0, g)),
            line(poles),
            line(poles),
            line(1),
            cube(length // 8),
            cube(poles),
            line(poles),
        ],
        out_specs=line(length),
        scratch_shapes=[
            pltpu.VMEM((length + 8, 128), jnp.float32),
            pltpu.VMEM((length, 128), jnp.float32),
        ],
        compiler_params=pltpu.CompilerParams(vmem_limit_bytes=16 << 20),
        name="modal_finish",
    )(edge, lower, upper, taps, rates, residues, skip.reshape(1, channels), u, starts, enter)


D = 4096
EPSILON = 1e-05
ROWS = 512
EXTRA = 16


def x_pairs(d):
    return [(c, c // 4 * 4 + (c + d) % 4) for c in range(16)]


def y_pairs(d):
    return [(c, (c + 4 * d) % 16) for c in range(16)]


def z_pairs(d):
    return [(t, (t + 2 * d) % 8) for t in range(8)]


def core_pairs():
    return [(t, t ^ 1) for t in range(8)]


def ring(a, axis, pairs):
    return [a] + [lax.ppermute(a, axis, pairs(-d)) for d in (1, 2, 3)]


def plane_gather(a, first, second):
    pieces = ring(a, "ctx", first)
    return ring(jnp.stack(pieces), "ctx", second)


def token_gather(a):
    pieces = ring(a, "tp", z_pairs)
    return (*pieces, *[lax.ppermute(p, "tp", core_pairs()) for p in pieces])


def mix_kernel(place_ref, *refs):
    acts, west, south, refs = refs[:8], refs[8:12], refs[12:16], refs[16:]
    residual_ref, out_ref, act_ref = refs
    y, x, z, core = (place_ref[n] for n in range(4))
    rows = act_ref.shape[1]
    for s in range(2):
        for dz in range(4):
            at = (z + dz) % 4 * 4 + (core ^ s) * 2
            for h in range(2):
                act_ref[at + h] = acts[4 * s + dz][:rows, h * 256 : h * 256 + 256]
    for side, weights in enumerate((west, south)):
        total = jnp.zeros((rows, 256), jnp.float32)
        for outer in range(4):
            left, right = [], []
            for inner in range(4):
                dy, dx = (outer, inner) if side == 0 else (inner, outer)
                left.append(act_ref[(y + dy) % 4 * 4 + (x + dx) % 4])
                right.append(weights[outer][inner])
            total = total + jnp.dot(
                jnp.concatenate(left, axis=1),
                jnp.concatenate(right, axis=0),
                preferred_element_type=jnp.float32,
            )
        lanes = slice(side * 256, side * 256 + 256)
        wide = residual_ref[:, lanes].astype(jnp.float32)
        out_ref[:, lanes] = (wide + total).astype(jnp.bfloat16)


def mix(place, acts, west, south, residual, at):
    rows, channels = ROWS, acts[0].shape[1]
    whole = lambda a: pl.BlockSpec(a.shape, lambda j, _: (0,) * a.ndim)
    return pl.pallas_call(
        mix_kernel,
        out_shape=jax.ShapeDtypeStruct((rows, channels), jnp.bfloat16),
        grid_spec=pltpu.PrefetchScalarGridSpec(
            num_scalar_prefetch=1,
            grid=(1,),
            in_specs=[whole(a) for a in (*acts, *west, *south)]
            + [pl.BlockSpec((rows, channels), lambda j, _: (at, 0))],
            out_specs=pl.BlockSpec((rows, channels), lambda j, _: (0, 0)),
            scratch_shapes=[pltpu.VMEM((16, rows, 256), jnp.bfloat16)],
        ),
        compiler_params=pltpu.CompilerParams(vmem_limit_bytes=40 << 20),
        name="mix",
    )(place, *acts, *west, *south, residual)


def collect_kernel(place_ref, *refs):
    acts, gains, (act_ref, scale_ref) = refs[:8], refs[8:16], refs[16:]
    z, core = place_ref[2], place_ref[3]
    squares = jnp.zeros(scale_ref.shape, jnp.float32)
    for s in range(2):
        for dz in range(4):
            wide = acts[4 * s + dz][...].astype(jnp.float32)
            gain = gains[4 * s + dz][:1, :].astype(jnp.float32)
            act_ref[(z + dz) % 4 * 2 + (core ^ s)] = (wide * gain).astype(jnp.bfloat16)
            wide = wide * wide
            for n in range(0, wide.shape[1], 128):
                squares = squares + wide[:, n : n + 128]
    total = jnp.sum(squares, axis=1, keepdims=True)
    scale_ref[...] = jnp.broadcast_to(lax.rsqrt(total / D + EPSILON), squares.shape)


def collect(place, acts, gains):
    rows, channels = acts[0].shape
    return pl.pallas_call(
        collect_kernel,
        out_shape=(
            jax.ShapeDtypeStruct((8, rows, channels), jnp.bfloat16),
            jax.ShapeDtypeStruct((rows, 128), jnp.float32),
        ),
        grid_spec=pltpu.PrefetchScalarGridSpec(
            num_scalar_prefetch=1,
            grid=(1,),
            in_specs=[pl.BlockSpec((rows, channels), lambda j, _: (0, 0)) for a in acts]
            + [pl.BlockSpec((EXTRA, channels), lambda j, _: (ROWS // EXTRA, 0)) for a in gains],
            out_specs=(
                pl.BlockSpec((8, rows, channels), lambda j, _: (0, 0, 0)),
                pl.BlockSpec((rows, 128), lambda j, _: (0, 0)),
            ),
        ),
        name="collect",
    )(place, *acts, *gains)


def project_kernel(act_ref, scale_ref, weight_ref, out_ref):
    left = jnp.concatenate([act_ref[n] for n in range(8)], axis=1)
    right = jnp.concatenate([weight_ref[n, 0] for n in range(16)], axis=0)
    total = jnp.dot(left, right, preferred_element_type=jnp.float32)
    scale = jnp.concatenate([scale_ref[...], scale_ref[...]], axis=1)
    out_ref[0] = (total * scale).astype(jnp.bfloat16)


def project(act, scale, weight, start, count):
    blocks, rows, channels = act.shape
    return pl.pallas_call(
        project_kernel,
        out_shape=jax.ShapeDtypeStruct((count, rows, channels), jnp.bfloat16),
        grid=(count, channels // 256),
        in_specs=[
            pl.BlockSpec((blocks, rows, channels), lambda m, n: (0, 0, 0)),
            pl.BlockSpec((rows, 128), lambda m, n: (0, 0)),
            pl.BlockSpec((16, 1, 256, 256), lambda m, n: (0, m + start, 0, n)),
        ],
        out_specs=pl.BlockSpec((1, rows, 256), lambda m, n: (m, 0, n)),
        name="project",
    )(act, scale, weight)


def on_device(
    qkv_first,
    short_first,
    medium_filter,
    out_weight,
    residual_in,
    norm_gain,
    in_weight,
    short_second,
    rates,
    residues,
    skip_gain,
):
    length = qkv_first.shape[1]
    c = lax.axis_index("ctx")
    t = lax.axis_index("tp")
    x, y, core, z = c % 4, c // 4, t % 2, t // 2
    place = jnp.stack([y, x, z, core]).astype(jnp.int32)
    ahead = [(i, i + 1) for i in range(15)]

    rim = lax.ppermute(qkv_first[:, length - HALO :], "ctx", ahead)

    packed = out_weight.reshape(2, 256, 256)
    odd = c % 2
    turned = []
    for k in range(2):
        pairs = []
        for cc in range(16):
            for tt in range(8):
                to = (2 * tt + (cc + k) % 2, cc // 2)
                pairs.append((cc * 8 + tt, to[0] * 8 + to[1]))
        mine = lax.dynamic_index_in_dim(packed, (odd + k) % 2, 0, False)
        turned.append(lax.ppermute(mine, ("ctx", "tp"), pairs))
    first = jnp.where(odd == 0, turned[0], turned[1])
    second = jnp.where(odd == 0, turned[1], turned[0])
    weight = lax.all_gather(in_weight, "ctx")
    out_west = plane_gather(first, x_pairs, y_pairs)
    out_south = plane_gather(second, y_pairs, x_pairs)

    filt = split_taps(medium_filter)
    upper = medium(qkv_first, 256, 1, qkv_first, 1, short_first, filt, norm_gain, EXTRA)
    upper_pieces = token_gather(upper)
    lower = medium(rim, HALO, 0, qkv_first, 0, short_first, filt, norm_gain, 0)
    lower_pieces = token_gather(lower)
    hidden_upper = mix(place, upper_pieces, out_west, out_south, residual_in, 1)
    hidden_upper_pieces = token_gather(hidden_upper)
    hidden_lower = mix(place, lower_pieces, out_west, out_south, residual_in, 0)
    hidden_lower_pieces = token_gather(hidden_lower)
    hidden = jnp.concatenate([hidden_lower, hidden_upper], axis=0)
    act, scale = collect(place, hidden_upper_pieces, upper_pieces)
    qkv_upper = project(act, scale, weight, 0, 3)
    edge = lax.ppermute(qkv_upper[:, ROWS - 16 :], "ctx", ahead)
    act, scale = collect(place, hidden_lower_pieces, upper_pieces)
    kv_lower = project(act, scale, weight, 1, 2)
    u, starts, end = modal_scan(edge, kv_lower, qkv_upper, short_second, rates)
    log_decay = -rates * length

    def decay(k):
        return jnp.exp(log_decay * k.astype(jnp.float32))

    along = [end] + [lax.ppermute(end, "ctx", x_pairs(-d)) for d in (1, 2, 3)]
    row = jnp.zeros_like(rates)
    enter = jnp.zeros_like(rates)
    for d, e in enumerate(along):
        at = (x + d) % 4
        wide = e.astype(jnp.float32)
        row = row + decay(3 - at) * wide
        enter = enter + jnp.where(at < x, decay(jnp.maximum(x - 1 - at, 0)), 0.0) * wide
    row = row.astype(jnp.bfloat16)
    for d in (1, 2, 3):
        e = lax.ppermute(row, "ctx", y_pairs(-d))
        at = (y + d) % 4
        enter = enter + jnp.where(
            at < y, decay(x + 4 * jnp.maximum(y - 1 - at, 0)), 0.0
        ) * e.astype(jnp.float32)
    q_lower = project(act, scale, weight, 0, 1)
    mixed = modal_finish(
        edge, q_lower, qkv_upper, short_second, rates, residues, skip_gain, u, starts, enter
    )
    return (hidden, mixed)


def solution(mesh):
    placed = (
        P(None, "ctx", "tp"),
        P(None, None, "tp"),
        P("tp", None),
        P("tp", "ctx"),
        P("ctx", "tp"),
        P("tp"),
        P(None, "ctx", "tp"),
        P(None, None, "tp"),
        P(None, "tp"),
        P(None, "tp"),
        P("tp"),
    )
    return jax.shard_map(
        on_device,
        mesh=mesh,
        in_specs=placed,
        out_specs=(P("ctx", "tp"), P("ctx", "tp")),
        check_vma=False,
    )
```

profile of v0, /device:TPU:28, one launch (start us, length us, event | category | flops | bytes accessed | tf_op | source)
XLA Modules:
  0.0 313.0 jit_solution(2982491377259257131)
XLA Ops:
  9.6 3.2 %collective-permute-start.9 = (bf16[256,256]{1,0:T(8,128)(2,1)}, bf16[256,256]{1,0:T(8,128)(2,1)}, u32[]{:S(2)}, u32[]{:S(2)}) collective-permute-start(bf16[256,256]{1,0:T(8,128)(2,1)} %get-tuple-element.18), channel_id=1, source_target_pairs={{0,8},{1,24},{2,40},{3,56},{4,72},{5,88},{6,104},{7,120},{8,0},{9,... | collective-permute-start | bytes 393224 | tf_op jit(solution)/shard_map/ppermute | solution.py:439
  12.8 6.0 %collective-permute-start.8 = (bf16[256,256]{1,0:T(8,128)(2,1)}, bf16[256,256]{1,0:T(8,128)(2,1)}, u32[]{:S(2)}, u32[]{:S(2)}) collective-permute-start(bf16[256,256]{1,0:T(8,128)(2,1)} %get-tuple-element.19), channel_id=1, source_target_pairs={{0,0},{1,16},{2,32},{3,48},{4,64},{5,80},{6,96},{7,112},{8,8},{9,2... | collective-permute-start | bytes 393224 | tf_op jit(solution)/shard_map/ppermute | solution.py:439
  22.0 4.2 %collective-permute-done.8 = bf16[256,256]{1,0:T(8,128)(2,1)} collective-permute-done((bf16[256,256]{1,0:T(8,128)(2,1)}, bf16[256,256]{1,0:T(8,128)(2,1)}, u32[]{:S(2)}, u32[]{:S(2)}) %collective-permute-start.8) | collective-permute-done | bytes 131104 | tf_op jit(solution)/shard_map/ppermute | solution.py:439
  28.0 4.1 %collective-permute-start.11 = (bf16[256,256]{1,0:T(8,128)(2,1)S(1)}, bf16[256,256]{1,0:T(8,128)(2,1)S(1)}, u32[]{:S(2)}, u32[]{:S(2)}) collective-permute-start(bf16[256,256]{1,0:T(8,128)(2,1)S(1)} %get-tuple-element.17), channel_id=1, source_target_pairs={{0,16},{8,24},{16,0},{24,8},{32,48},{40,56},{48,32},{56,40},{64,80... | collective-permute-start | bytes 393224 | tf_op jit(solution)/shard_map/ppermute | solution.py:285
  34.8 3.6 %collective-permute-done.12 = bf16[256,256]{1,0:T(8,128)(2,1)S(1)} collective-permute-done((bf16[256,256]{1,0:T(8,128)(2,1)S(1)}, bf16[256,256]{1,0:T(8,128)(2,1)S(1)}, u32[]{:S(2)}, u32[]{:S(2)}) %collective-permute-start.12) | collective-permute-done | bytes 131104 | tf_op jit(solution)/shard_map/ppermute | solution.py:285
  40.2 10.9 %medium.3.refs_0_.refs_8_ = bf16[528,512]{1,0:T(8,128)(2,1)S(1)} custom-call(bf16[3,1024,512]{2,1,0:T(8,128)(2,1)S(1)} %copy-done, bf16[3,1024,512]{2,1,0:T(8,128)(2,1)S(1)} %copy-done, f32[3,3,512]{2,1,0:T(4,128)S(1)} %copy-done.47, f32[9,32,512]{2,1,0:T(8,128)S(1)} %add_dynamic-update-slice_fusion.filt_ref, bf16[1,512]{1,0:T(2,128)(2,1)S(1)} %reshape.109.gain_ref), custom_call_target="tpu_custom_call" | custom-call | tf_op jit(solution)/shard_map/medium/pallas_call | solution.py:82
  52.2 3.3 %collective-permute-start = (bf16[3,144,512]{2,1,0:T(8,128)(2,1)S(1)}, bf16[3,144,512]{2,1,0:T(8,128)(2,1)S(1)}, u32[]{:S(2)}, u32[]{:S(2)}) collective-permute-start(bf16[3,144,512]{2,1,0:T(8,128)(2,1)S(1)} %slice.22), channel_id=1, source_target_pairs={{0,8},{8,16},{16,24},{24,32},{32,40},{40,48},{48,56},{56,64},{64,7... | collective-permute-start | bytes 1327112 | tf_op jit(solution)/shard_map/ppermute | solution.py:427
  55.8 19.4 %collective-permute-done.prev_ref = bf16[3,144,512]{2,1,0:T(8,128)(2,1)S(1)} collective-permute-done((bf16[3,144,512]{2,1,0:T(8,128)(2,1)S(1)}, bf16[3,144,512]{2,1,0:T(8,128)(2,1)S(1)}, u32[]{:S(2)}, u32[]{:S(2)}) %collective-permute-start) | collective-permute-done | bytes 442400 | tf_op jit(solution)/shard_map/ppermute | solution.py:427
  77.1 3.0 collective-permute-start.14
  83.0 3.2 %collective-permute-start.19 = (bf16[4,256,256]{2,1,0:T(8,128)(2,1)S(1)}, bf16[4,256,256]{2,1,0:T(8,128)(2,1)S(1)}, u32[]{:S(2)}, u32[]{:S(2)}) collective-permute-start(bf16[4,256,256]{2,1,0:T(8,128)(2,1)S(1)} %pad_maximum_fusion.2.refs_12_), channel_id=1, source_target_pairs={{0,24},{8,0},{16,8},{24,16},{32,56},{40,32},{48,40},{56,48},{64,88... | collective-permute-start | bytes 1572872 | tf_op jit(solution)/shard_map/ppermute | solution.py:285
  87.0 3.5 %collective-permute-start.20 = (bf16[4,256,256]{2,1,0:T(8,128)(2,1)S(1)}, bf16[4,256,256]{2,1,0:T(8,128)(2,1)S(1)}, u32[]{:S(2)}, u32[]{:S(2)}) collective-permute-start(bf16[4,256,256]{2,1,0:T(8,128)(2,1)S(1)} %pad_maximum_fusion.2.refs_12_), channel_id=1, source_target_pairs={{0,16},{8,24},{16,0},{24,8},{32,48},{40,56},{48,32},{56,40},{64,80... | collective-permute-start | bytes 1572872 | tf_op jit(solution)/shard_map/ppermute | solution.py:285
  90.6 11.6 %collective-permute-done.13.refs_9_ = bf16[4,256,256]{2,1,0:T(8,128)(2,1)S(1)} collective-permute-done((bf16[4,256,256]{2,1,0:T(8,128)(2,1)S(1)}, bf16[4,256,256]{2,1,0:T(8,128)(2,1)S(1)}, u32[]{:S(2)}, u32[]{:S(2)}) %collective-permute-start.13) | collective-permute-done | bytes 524320 | tf_op jit(solution)/shard_map/ppermute | solution.py:285
  103.0 4.1 %collective-permute-start.21 = (bf16[4,256,256]{2,1,0:T(8,128)(2,1)S(1)}, bf16[4,256,256]{2,1,0:T(8,128)(2,1)S(1)}, u32[]{:S(2)}, u32[]{:S(2)}) collective-permute-start(bf16[4,256,256]{2,1,0:T(8,128)(2,1)S(1)} %pad_maximum_fusion.2.refs_12_), channel_id=1, source_target_pairs={{0,8},{8,16},{16,24},{24,0},{32,40},{40,48},{48,56},{56,32},{64,72... | collective-permute-start | bytes 1572872 | tf_op jit(solution)/shard_map/ppermute | solution.py:285
  107.8 11.3 %medium.2.refs_0_ = bf16[512,512]{1,0:T(8,128)(2,1)} custom-call(bf16[3,144,512]{2,1,0:T(8,128)(2,1)S(1)} %collective-permute-done.prev_ref, bf16[3,1024,512]{2,1,0:T(8,128)(2,1)S(1)} %copy-done, f32[3,3,512]{2,1,0:T(4,128)S(1)} %copy-done.47, f32[9,32,512]{2,1,0:T(8,128)S(1)} %add_dynamic-update-slice_fusion.filt_ref, bf16[1,512]{1,0:T(2,128)(2,1)S(1)} %reshape.109.gain_ref), custom_call_target="tpu_custom_call" | custom-call | tf_op jit(solution)/shard_map/medium/pallas_call | solution.py:82
  119.1 6.4 %collective-permute-done.14.refs_10_ = bf16[4,256,256]{2,1,0:T(8,128)(2,1)S(1)} collective-permute-done((bf16[4,256,256]{2,1,0:T(8,128)(2,1)S(1)}, bf16[4,256,256]{2,1,0:T(8,128)(2,1)S(1)}, u32[]{:S(2)}, u32[]{:S(2)}) %collective-permute-start.14) | collective-permute-done | bytes 524320 | tf_op jit(solution)/shard_map/ppermute | solution.py:285
  135.3 14.7 %collective-permute-done.1.refs_1_ = bf16[512,512]{1,0:T(8,128)(2,1)S(1)} collective-permute-done((bf16[512,512]{1,0:T(8,128)(2,1)}, bf16[512,512]{1,0:T(8,128)(2,1)S(1)}, u32[]{:S(2)}, u32[]{:S(2)}) %collective-permute-start.1) | collective-permute-done | bytes 524320 | tf_op jit(solution)/shard_map/ppermute | solution.py:285
  150.6 7.8 %collective-permute-done.3.refs_3_ = bf16[512,512]{1,0:T(8,128)(2,1)} collective-permute-done((bf16[512,512]{1,0:T(8,128)(2,1)}, bf16[512,512]{1,0:T(8,128)(2,1)}, u32[]{:S(2)}, u32[]{:S(2)}) %collective-permute-start.3) | collective-permute-done | bytes 524320 | tf_op jit(solution)/shard_map/ppermute | solution.py:285
  171.8 4.9 %mix.3.refs_0_ = bf16[512,512]{1,0:T(8,128)(2,1)S(1)} custom-call(s32[4]{0:T(128)S(1)} %pad_add_fusion.place_ref, bf16[528,512]{1,0:T(8,128)(2,1)S(1)} %copy-done.3, bf16[528,512]{1,0:T(8,128)(2,1)S(1)} %copy-done.5, bf16[528,512]{1,0:T(8,128)(2,1)} %collective-permute-done.23.refs_2_.refs_10_, bf16[528,512]{1,0:T(8,128)(2,1)} %collective-permute-done.24.refs_3_.refs_11_, ...), custom_call_target="tpu_custom_call" | custom-call | tf_op jit(solution)/shard_map/mix/pallas_call | solution.py:329
  180.1 4.8 %mix.2.refs_0_ = bf16[512,512]{1,0:T(8,128)(2,1)S(1)} custom-call(s32[4]{0:T(128)S(1)} %pad_add_fusion.place_ref, bf16[512,512]{1,0:T(8,128)(2,1)} %medium.2.refs_0_, bf16[512,512]{1,0:T(8,128)(2,1)S(1)} %collective-permute-done.1.refs_1_, bf16[512,512]{1,0:T(8,128)(2,1)S(1)} %copy-done.45, bf16[512,512]{1,0:T(8,128)(2,1)} %collective-permute-done.3.refs_3_, ...), custom_call_target="tpu_custom_call" | custom-call | tf_op jit(solution)/shard_map/mix/pallas_call | solution.py:329
  187.7 3.9 %collective-permute-done.29.refs_1_ = bf16[512,512]{1,0:T(8,128)(2,1)S(1)} collective-permute-done((bf16[512,512]{1,0:T(8,128)(2,1)S(1)}, bf16[512,512]{1,0:T(8,128)(2,1)S(1)}, u32[]{:S(2)}, u32[]{:S(2)}) %collective-permute-start.29) | collective-permute-done | bytes 524320 | tf_op jit(solution)/shard_map/ppermute | solution.py:285
  193.8 8.8 %collective-permute-start.39 = (bf16[512,512]{1,0:T(8,128)(2,1)S(1)}, bf16[512,512]{1,0:T(8,128)(2,1)}, u32[]{:S(2)}, u32[]{:S(2)}) collective-permute-start(bf16[512,512]{1,0:T(8,128)(2,1)S(1)} %mix.2.refs_0_), channel_id=1, source_target_pairs={{0,2},{1,3},{2,4},{3,5},{4,6},{5,7},{6,0},{7,1},{8,10},{9,11},{10,... | collective-permute-start | bytes 1572872 | tf_op jit(solution)/shard_map/ppermute | solution.py:285
  205.4 8.7 %collective-permute-done.37.refs_1_ = bf16[512,512]{1,0:T(8,128)(2,1)S(1)} collective-permute-done((bf16[512,512]{1,0:T(8,128)(2,1)S(1)}, bf16[512,512]{1,0:T(8,128)(2,1)S(1)}, u32[]{:S(2)}, u32[]{:S(2)}) %collective-permute-start.37) | collective-permute-done | bytes 524320 | tf_op jit(solution)/shard_map/ppermute | solution.py:285
  216.3 10.4 %collective-permute-done.39.refs_3_ = bf16[512,512]{1,0:T(8,128)(2,1)} collective-permute-done((bf16[512,512]{1,0:T(8,128)(2,1)S(1)}, bf16[512,512]{1,0:T(8,128)(2,1)}, u32[]{:S(2)}, u32[]{:S(2)}) %collective-permute-start.39) | collective-permute-done | bytes 524320 | tf_op jit(solution)/shard_map/ppermute | solution.py:285
  228.1 6.7 %collect.2 = (bf16[8,512,512]{2,1,0:T(8,128)(2,1)}, f32[512,128]{1,0:T(8,128)}) custom-call(s32[4]{0:T(128)} %copy-done.50, bf16[512,512]{1,0:T(8,128)(2,1)} %copy-done.17, bf16[512,512]{1,0:T(8,128)(2,1)} %copy-done.52, bf16[512,512]{1,0:T(8,128)(2,1)} %copy-done.54, bf16[512,512]{1,0:T(8,128)(2,1)} %copy-done.56, bf16[512,512]{1,0:T(8,128)(2,1)} %copy-done.57, ...), custom_call_target="tpu_custom_call" | custom-call | tf_op jit(solution)/shard_map/collect/pallas_call | solution.py:363
  234.8 12.3 %project.3.upper_ref = bf16[3,512,512]{2,1,0:T(8,128)(2,1)} custom-call(bf16[8,512,512]{2,1,0:T(8,128)(2,1)} %get-tuple-element.9.act_ref, f32[512,128]{1,0:T(8,128)} %get-tuple-element.10.scale_ref, bf16[16,3,256,512]{3,2,1,0:T(8,128)(2,1)} %bitcast.70), custom_call_target="tpu_custom_call" | custom-call | tf_op jit(solution)/shard_map/project/pallas_call | solution.py:393
  247.9 3.9 %collective-permute-start.36 = (bf16[3,16,512]{2,1,0:T(8,128)(2,1)S(1)}, bf16[3,16,512]{2,1,0:T(8,128)(2,1)S(1)}, u32[]{:S(2)}, u32[]{:S(2)}) collective-permute-start(bf16[3,16,512]{2,1,0:T(8,128)(2,1)S(1)} %slice.32), channel_id=1, source_target_pairs={{0,8},{8,16},{16,24},{24,32},{32,40},{40,48},{48,56},{56,64},{64,7... | collective-permute-start | bytes 147464 | tf_op jit(solution)/shard_map/ppermute | solution.py:458
  251.8 6.7 %collect.3 = (bf16[8,512,512]{2,1,0:T(8,128)(2,1)}, f32[512,128]{1,0:T(8,128)}) custom-call(s32[4]{0:T(128)} %copy-done.50, bf16[512,512]{1,0:T(8,128)(2,1)} %copy-done.19, bf16[512,512]{1,0:T(8,128)(2,1)} %copy-done.53, bf16[512,512]{1,0:T(8,128)(2,1)} %copy-done.55, bf16[512,512]{1,0:T(8,128)(2,1)} %collective-permute-done.39.refs_3_, ...), custom_call_target="tpu_custom_call" | custom-call | tf_op jit(solution)/shard_map/collect/pallas_call | solution.py:363
  258.5 9.3 %project.5.lower_ref = bf16[2,512,512]{2,1,0:T(8,128)(2,1)} custom-call(bf16[8,512,512]{2,1,0:T(8,128)(2,1)} %get-tuple-element.11.act_ref, f32[512,128]{1,0:T(8,128)} %get-tuple-element.12.scale_ref, bf16[16,3,256,512]{3,2,1,0:T(8,128)(2,1)} %bitcast.71), custom_call_target="tpu_custom_call" | custom-call | tf_op jit(solution)/shard_map/project/pallas_call | solution.py:393
  269.2 6.4 %modal_scan.1 = (f32[128,8,512]{2,1,0:T(8,128)S(1)}, f32[16,8,512]{2,1,0:T(8,128)S(1)}, bf16[16,512]{1,0:T(8,128)(2,1)S(1)}) custom-call(bf16[3,16,512]{2,1,0:T(8,128)(2,1)S(1)} %collective-permute-done.36.edge_ref, bf16[2,512,512]{2,1,0:T(8,128)(2,1)S(1)} %copy-done.22, bf16[3,512,512]{2,1,0:T(8,128)(2,1)S(1)} %copy-done.1, f32[3,3,512]{2,1,0:T(4,128)S(1)} %copy-done.48, ...), custom_call_target="tpu_custom_call" | custom-call | tf_op jit(solution)/shard_map/modal_scan/pallas_call | solution.py:171
  282.4 5.3 %collective-permute-start.49 = (bf16[16,512]{1,0:T(8,128)(2,1)S(1)}, bf16[16,512]{1,0:T(8,128)(2,1)S(1)}, u32[]{:S(2)}, u32[]{:S(2)}) collective-permute-start(bf16[16,512]{1,0:T(8,128)(2,1)S(1)} %fusion.15), channel_id=1, source_target_pairs={{0,32},{8,40},{16,48},{24,56},{32,64},{40,72},{48,80},{56,88},{64,... | collective-permute-start | bytes 49160 | tf_op jit(solution)/shard_map/ppermute | solution.py:477
  289.7 6.2 %project.4.lower_ref = bf16[1,512,512]{2,1,0:T(8,128)(2,1)} custom-call(bf16[8,512,512]{2,1,0:T(8,128)(2,1)} %get-tuple-element.11.act_ref, f32[512,128]{1,0:T(8,128)} %get-tuple-element.12.scale_ref, bf16[16,3,256,512]{3,2,1,0:T(8,128)(2,1)} %bitcast.72), custom_call_target="tpu_custom_call" | custom-call | tf_op jit(solution)/shard_map/project/pallas_call | solution.py:393
  298.6 7.5 %modal_finish.1 = bf16[1024,512]{1,0:T(8,128)(2,1)} custom-call(bf16[3,16,512]{2,1,0:T(8,128)(2,1)S(1)} %collective-permute-done.36.edge_ref, bf16[1,512,512]{2,1,0:T(8,128)(2,1)S(1)} %copy-done.43, bf16[3,512,512]{2,1,0:T(8,128)(2,1)S(1)} %copy-done.1, f32[3,3,512]{2,1,0:T(4,128)S(1)} %copy-done.48, f32[16,512]{1,0:T(8,128)S(1)} %copy-done.46, ...), custom_call_target="tpu_custom_call" | custom-call | tf_op jit(solution)/shard_map/modal_finish/pallas_call | solution.py:236
  (228 shorter events, 72.3 us)
Async XLA Ops:
  7.2 227.6 %all-gather.3.cloned.1.call-start = ((), (), s32[]{:S(2)}) async-start(), calls=%async_computation | async-start | bytes 13369344 | tf_op jit(solution)/shard_map/all_gather | solution.py:442
  28.0 23.0 %collective-permute-start.11 = (bf16[256,256]{1,0:T(8,128)(2,1)S(1)}, bf16[256,256]{1,0:T(8,128)(2,1)S(1)}, u32[]{:S(2)}, u32[]{:S(2)}) collective-permute-start(bf16[256,256]{1,0:T(8,128)(2,1)S(1)} %get-tuple-element.17), channel_id=1, source_target_pairs={{0,16},{8,24},{16,0},{24,8},{32,48},{40,56},{48,32},{56,40},{64,80... | collective-permute-start | bytes 393224 | tf_op jit(solution)/shard_map/ppermute | solution.py:285
  33.9 21.7 %collective-permute-start.17 = (bf16[256,256]{1,0:T(8,128)(2,1)S(1)}, bf16[256,256]{1,0:T(8,128)(2,1)S(1)}, u32[]{:S(2)}, u32[]{:S(2)}) collective-permute-start(bf16[256,256]{1,0:T(8,128)(2,1)S(1)} %get-tuple-element.16), channel_id=1, source_target_pairs={{0,64},{8,72},{16,80},{24,88},{32,96},{40,104},{48,112},{56,120},{... | collective-permute-start | bytes 393224 | tf_op jit(solution)/shard_map/ppermute | solution.py:285
  51.1 26.1 %collective-permute-start.22 = (bf16[528,512]{1,0:T(8,128)(2,1)S(1)}, bf16[528,512]{1,0:T(8,128)(2,1)S(1)}, u32[]{:S(2)}, u32[]{:S(2)}) collective-permute-start(bf16[528,512]{1,0:T(8,128)(2,1)S(1)} %medium.3.refs_0_.refs_8_), channel_id=1, source_target_pairs={{0,6},{1,7},{2,0},{3,1},{4,2},{5,3},{6,4},{7,5},{8,14},{9,15},{10,... | collective-permute-start | bytes 1622024 | tf_op jit(solution)/shard_map/ppermute | solution.py:285
  52.1 28.0 %collective-permute-start.23 = (bf16[528,512]{1,0:T(8,128)(2,1)S(1)}, bf16[528,512]{1,0:T(8,128)(2,1)}, u32[]{:S(2)}, u32[]{:S(2)}) collective-permute-start(bf16[528,512]{1,0:T(8,128)(2,1)S(1)} %medium.3.refs_0_.refs_8_), channel_id=1, source_target_pairs={{0,4},{1,5},{2,6},{3,7},{4,0},{5,1},{6,2},{7,3},{8,12},{9,13},{10,... | collective-permute-start | bytes 1622024 | tf_op jit(solution)/shard_map/ppermute | solution.py:285
  52.2 23.0 %collective-permute-start = (bf16[3,144,512]{2,1,0:T(8,128)(2,1)S(1)}, bf16[3,144,512]{2,1,0:T(8,128)(2,1)S(1)}, u32[]{:S(2)}, u32[]{:S(2)}) collective-permute-start(bf16[3,144,512]{2,1,0:T(8,128)(2,1)S(1)} %slice.22), channel_id=1, source_target_pairs={{0,8},{8,16},{16,24},{24,32},{32,40},{40,48},{48,56},{56,64},{64,7... | collective-permute-start | bytes 1327112 | tf_op jit(solution)/shard_map/ppermute | solution.py:427
  55.5 27.4 %collective-permute-start.24 = (bf16[528,512]{1,0:T(8,128)(2,1)S(1)}, bf16[528,512]{1,0:T(8,128)(2,1)}, u32[]{:S(2)}, u32[]{:S(2)}) collective-permute-start(bf16[528,512]{1,0:T(8,128)(2,1)S(1)} %medium.3.refs_0_.refs_8_), channel_id=1, source_target_pairs={{0,2},{1,3},{2,4},{3,5},{4,6},{5,7},{6,0},{7,1},{8,10},{9,11},{10,... | collective-permute-start | bytes 1622024 | tf_op jit(solution)/shard_map/ppermute | solution.py:285
  55.6 30.6 %collective-permute-start.25 = (bf16[528,512]{1,0:T(8,128)(2,1)S(1)}, bf16[528,512]{1,0:T(8,128)(2,1)S(1)}, u32[]{:S(2)}, u32[]{:S(2)}) collective-permute-start(bf16[528,512]{1,0:T(8,128)(2,1)S(1)} %medium.3.refs_0_.refs_8_), channel_id=1, source_target_pairs={{0,1},{1,0},{2,3},{3,2},{4,5},{5,4},{6,7},{7,6},{8,9},{9,8},{10,11... | collective-permute-start | bytes 1622024 | tf_op jit(solution)/shard_map/ppermute | solution.py:295
  75.2 27.0 %collective-permute-start.13 = (bf16[4,256,256]{2,1,0:T(8,128)(2,1)S(1)}, bf16[4,256,256]{2,1,0:T(8,128)(2,1)S(1)}, u32[]{:S(2)}, u32[]{:S(2)}) collective-permute-start(bf16[4,256,256]{2,1,0:T(8,128)(2,1)S(1)} %pad_maximum_fusion.1.refs_8_), channel_id=1, source_target_pairs={{0,96},{8,104},{16,112},{24,120},{32,0},{40,8},{48,16},{56,24},{64... | collective-permute-start | bytes 1572872 | tf_op jit(solution)/shard_map/ppermute | solution.py:285
  77.1 48.4 %collective-permute-start.14 = (bf16[4,256,256]{2,1,0:T(8,128)(2,1)S(1)}, bf16[4,256,256]{2,1,0:T(8,128)(2,1)S(1)}, u32[]{:S(2)}, u32[]{:S(2)}) collective-permute-start(bf16[4,256,256]{2,1,0:T(8,128)(2,1)S(1)} %pad_maximum_fusion.1.refs_8_), channel_id=1, source_target_pairs={{0,64},{8,72},{16,80},{24,88},{32,96},{40,104},{48,112},{56,120},{... | collective-permute-start | bytes 1572872 | tf_op jit(solution)/shard_map/ppermute | solution.py:285
  80.1 49.2 %collective-permute-start.15 = (bf16[4,256,256]{2,1,0:T(8,128)(2,1)S(1)}, bf16[4,256,256]{2,1,0:T(8,128)(2,1)S(1)}, u32[]{:S(2)}, u32[]{:S(2)}) collective-permute-start(bf16[4,256,256]{2,1,0:T(8,128)(2,1)S(1)} %pad_maximum_fusion.1.refs_8_), channel_id=1, source_target_pairs={{0,32},{8,40},{16,48},{24,56},{32,64},{40,72},{48,80},{56,88},{64,... | collective-permute-start | bytes 1572872 | tf_op jit(solution)/shard_map/ppermute | solution.py:285
  83.0 47.2 %collective-permute-start.19 = (bf16[4,256,256]{2,1,0:T(8,128)(2,1)S(1)}, bf16[4,256,256]{2,1,0:T(8,128)(2,1)S(1)}, u32[]{:S(2)}, u32[]{:S(2)}) collective-permute-start(bf16[4,256,256]{2,1,0:T(8,128)(2,1)S(1)} %pad_maximum_fusion.2.refs_12_), channel_id=1, source_target_pairs={{0,24},{8,0},{16,8},{24,16},{32,56},{40,32},{48,40},{56,48},{64,88... | collective-permute-start | bytes 1572872 | tf_op jit(solution)/shard_map/ppermute | solution.py:285
  87.0 44.0 %collective-permute-start.20 = (bf16[4,256,256]{2,1,0:T(8,128)(2,1)S(1)}, bf16[4,256,256]{2,1,0:T(8,128)(2,1)S(1)}, u32[]{:S(2)}, u32[]{:S(2)}) collective-permute-start(bf16[4,256,256]{2,1,0:T(8,128)(2,1)S(1)} %pad_maximum_fusion.2.refs_12_), channel_id=1, source_target_pairs={{0,16},{8,24},{16,0},{24,8},{32,48},{40,56},{48,32},{56,40},{64,80... | collective-permute-start | bytes 1572872 | tf_op jit(solution)/shard_map/ppermute | solution.py:285
  103.0 31.6 %collective-permute-start.21 = (bf16[4,256,256]{2,1,0:T(8,128)(2,1)S(1)}, bf16[4,256,256]{2,1,0:T(8,128)(2,1)S(1)}, u32[]{:S(2)}, u32[]{:S(2)}) collective-permute-start(bf16[4,256,256]{2,1,0:T(8,128)(2,1)S(1)} %pad_maximum_fusion.2.refs_12_), channel_id=1, source_target_pairs={{0,8},{8,16},{16,24},{24,0},{32,40},{40,48},{48,56},{56,32},{64,72... | collective-permute-start | bytes 1572872 | tf_op jit(solution)/shard_map/ppermute | solution.py:285
  126.3 23.7 %collective-permute-start.1 = (bf16[512,512]{1,0:T(8,128)(2,1)}, bf16[512,512]{1,0:T(8,128)(2,1)S(1)}, u32[]{:S(2)}, u32[]{:S(2)}) collective-permute-start(bf16[512,512]{1,0:T(8,128)(2,1)} %medium.2.refs_0_), channel_id=1, source_target_pairs={{0,6},{1,7},{2,0},{3,1},{4,2},{5,3},{6,4},{7,5},{8,14},{9,15},{10,... | collective-permute-start | bytes 1572872 | tf_op jit(solution)/shard_map/ppermute | solution.py:285
  130.1 28.3 %collective-permute-start.26 = (bf16[528,512]{1,0:T(8,128)(2,1)S(1)}, bf16[528,512]{1,0:T(8,128)(2,1)S(1)}, u32[]{:S(2)}, u32[]{:S(2)}) collective-permute-start(bf16[528,512]{1,0:T(8,128)(2,1)S(1)} %collective-permute-done.22.refs_1_.refs_9_), channel_id=1, source_target_pairs={{0,1},{1,0},{2,3},{3,2},{4,5},{5,4},{6,7},{7,6},{8,9},{9,8},{10,11... | collective-permute-start | bytes 1622024 | tf_op jit(solution)/shard_map/ppermute | solution.py:295
  131.8 26.5 %collective-permute-start.3 = (bf16[512,512]{1,0:T(8,128)(2,1)}, bf16[512,512]{1,0:T(8,128)(2,1)}, u32[]{:S(2)}, u32[]{:S(2)}) collective-permute-start(bf16[512,512]{1,0:T(8,128)(2,1)} %medium.2.refs_0_), channel_id=1, source_target_pairs={{0,2},{1,3},{2,4},{3,5},{4,6},{5,7},{6,0},{7,1},{8,10},{9,11},{10,... | collective-permute-start | bytes 1572872 | tf_op jit(solution)/shard_map/ppermute | solution.py:285
  135.3 23.5 %collective-permute-start.27 = (bf16[528,512]{1,0:T(8,128)(2,1)}, bf16[528,512]{1,0:T(8,128)(2,1)S(1)}, u32[]{:S(2)}, u32[]{:S(2)}) collective-permute-start(bf16[528,512]{1,0:T(8,128)(2,1)} %collective-permute-done.23.refs_2_.refs_10_), channel_id=1, source_target_pairs={{0,1},{1,0},{2,3},{3,2},{4,5},{5,4},{6,7},{7,6},{8,9},{9,8},{10,11... | collective-permute-start | bytes 1622024 | tf_op jit(solution)/shard_map/ppermute | solution.py:295
  150.1 27.4 %collective-permute-start.4 = (bf16[512,512]{1,0:T(8,128)(2,1)}, bf16[512,512]{1,0:T(8,128)(2,1)}, u32[]{:S(2)}, u32[]{:S(2)}) collective-permute-start(bf16[512,512]{1,0:T(8,128)(2,1)} %medium.2.refs_0_), channel_id=1, source_target_pairs={{0,1},{1,0},{2,3},{3,2},{4,5},{5,4},{6,7},{7,6},{8,9},{9,8},{10,11... | collective-permute-start | bytes 1572872 | tf_op jit(solution)/shard_map/ppermute | solution.py:295
  158.4 20.5 %collective-permute-start.6 = (bf16[512,512]{1,0:T(8,128)(2,1)S(1)}, bf16[512,512]{1,0:T(8,128)(2,1)}, u32[]{:S(2)}, u32[]{:S(2)}) collective-permute-start(bf16[512,512]{1,0:T(8,128)(2,1)S(1)} %collective-permute-done.2.refs_2_), channel_id=1, source_target_pairs={{0,1},{1,0},{2,3},{3,2},{4,5},{5,4},{6,7},{7,6},{8,9},{9,8},{10,11... | collective-permute-start | bytes 1572872 | tf_op jit(solution)/shard_map/ppermute | solution.py:295
  158.8 20.1 %collective-permute-start.7 = (bf16[512,512]{1,0:T(8,128)(2,1)}, bf16[512,512]{1,0:T(8,128)(2,1)S(1)}, u32[]{:S(2)}, u32[]{:S(2)}) collective-permute-start(bf16[512,512]{1,0:T(8,128)(2,1)} %collective-permute-done.3.refs_3_), channel_id=1, source_target_pairs={{0,1},{1,0},{2,3},{3,2},{4,5},{5,4},{6,7},{7,6},{8,9},{9,8},{10,11... | collective-permute-start | bytes 1572872 | tf_op jit(solution)/shard_map/ppermute | solution.py:295
  177.7 27.2 %collective-permute-start.31 = (bf16[512,512]{1,0:T(8,128)(2,1)S(1)}, bf16[512,512]{1,0:T(8,128)(2,1)S(1)}, u32[]{:S(2)}, u32[]{:S(2)}) collective-permute-start(bf16[512,512]{1,0:T(8,128)(2,1)S(1)} %mix.3.refs_0_), channel_id=1, source_target_pairs={{0,2},{1,3},{2,4},{3,5},{4,6},{5,7},{6,0},{7,1},{8,10},{9,11},{10,... | collective-permute-start | bytes 1572872 | tf_op jit(solution)/shard_map/ppermute | solution.py:285
  178.9 26.0 %collective-permute-start.32 = (bf16[512,512]{1,0:T(8,128)(2,1)S(1)}, bf16[512,512]{1,0:T(8,128)(2,1)S(1)}, u32[]{:S(2)}, u32[]{:S(2)}) collective-permute-start(bf16[512,512]{1,0:T(8,128)(2,1)S(1)} %mix.3.refs_0_), channel_id=1, source_target_pairs={{0,1},{1,0},{2,3},{3,2},{4,5},{5,4},{6,7},{7,6},{8,9},{9,8},{10,11... | collective-permute-start | bytes 1572872 | tf_op jit(solution)/shard_map/ppermute | solution.py:295
  184.9 29.2 %collective-permute-start.37 = (bf16[512,512]{1,0:T(8,128)(2,1)S(1)}, bf16[512,512]{1,0:T(8,128)(2,1)S(1)}, u32[]{:S(2)}, u32[]{:S(2)}) collective-permute-start(bf16[512,512]{1,0:T(8,128)(2,1)S(1)} %mix.2.refs_0_), channel_id=1, source_target_pairs={{0,6},{1,7},{2,0},{3,1},{4,2},{5,3},{6,4},{7,5},{8,14},{9,15},{10,... | collective-permute-start | bytes 1572872 | tf_op jit(solution)/shard_map/ppermute | solution.py:285
  191.6 24.7 %collective-permute-start.38 = (bf16[512,512]{1,0:T(8,128)(2,1)S(1)}, bf16[512,512]{1,0:T(8,128)(2,1)S(1)}, u32[]{:S(2)}, u32[]{:S(2)}) collective-permute-start(bf16[512,512]{1,0:T(8,128)(2,1)S(1)} %mix.2.refs_0_), channel_id=1, source_target_pairs={{0,4},{1,5},{2,6},{3,7},{4,0},{5,1},{6,2},{7,3},{8,12},{9,13},{10,... | collective-permute-start | bytes 1572872 | tf_op jit(solution)/shard_map/ppermute | solution.py:285
  193.8 32.9 %collective-permute-start.39 = (bf16[512,512]{1,0:T(8,128)(2,1)S(1)}, bf16[512,512]{1,0:T(8,128)(2,1)}, u32[]{:S(2)}, u32[]{:S(2)}) collective-permute-start(bf16[512,512]{1,0:T(8,128)(2,1)S(1)} %mix.2.refs_0_), channel_id=1, source_target_pairs={{0,2},{1,3},{2,4},{3,5},{4,6},{5,7},{6,0},{7,1},{8,10},{9,11},{10,... | collective-permute-start | bytes 1572872 | tf_op jit(solution)/shard_map/ppermute | solution.py:285
  204.9 21.8 %collective-permute-start.33 = (bf16[512,512]{1,0:T(8,128)(2,1)S(1)}, bf16[512,512]{1,0:T(8,128)(2,1)S(1)}, u32[]{:S(2)}, u32[]{:S(2)}) collective-permute-start(bf16[512,512]{1,0:T(8,128)(2,1)S(1)} %collective-permute-done.29.refs_1_), channel_id=1, source_target_pairs={{0,1},{1,0},{2,3},{3,2},{4,5},{5,4},{6,7},{7,6},{8,9},{9,8},{10,11... | collective-permute-start | bytes 1572872 | tf_op jit(solution)/shard_map/ppermute | solution.py:295
  204.9 22.3 %collective-permute-start.34 = (bf16[512,512]{1,0:T(8,128)(2,1)S(1)}, bf16[512,512]{1,0:T(8,128)(2,1)S(1)}, u32[]{:S(2)}, u32[]{:S(2)}) collective-permute-start(bf16[512,512]{1,0:T(8,128)(2,1)S(1)} %collective-permute-done.30.refs_2_), channel_id=1, source_target_pairs={{0,1},{1,0},{2,3},{3,2},{4,5},{5,4},{6,7},{7,6},{8,9},{9,8},{10,11... | collective-permute-start | bytes 1572872 | tf_op jit(solution)/shard_map/ppermute | solution.py:295
  216.3 35.5 %collective-permute-start.40 = (bf16[512,512]{1,0:T(8,128)(2,1)S(1)}, bf16[512,512]{1,0:T(8,128)(2,1)}, u32[]{:S(2)}, u32[]{:S(2)}) collective-permute-start(bf16[512,512]{1,0:T(8,128)(2,1)S(1)} %mix.2.refs_0_), channel_id=1, source_target_pairs={{0,1},{1,0},{2,3},{3,2},{4,5},{5,4},{6,7},{7,6},{8,9},{9,8},{10,11... | collective-permute-start | bytes 1572872 | tf_op jit(solution)/shard_map/ppermute | solution.py:295
  226.7 25.1 %collective-permute-start.41 = (bf16[512,512]{1,0:T(8,128)(2,1)S(1)}, bf16[512,512]{1,0:T(8,128)(2,1)}, u32[]{:S(2)}, u32[]{:S(2)}) collective-permute-start(bf16[512,512]{1,0:T(8,128)(2,1)S(1)} %collective-permute-done.37.refs_1_), channel_id=1, source_target_pairs={{0,1},{1,0},{2,3},{3,2},{4,5},{5,4},{6,7},{7,6},{8,9},{9,8},{10,11... | collective-permute-start | bytes 1572872 | tf_op jit(solution)/shard_map/ppermute | solution.py:295
  226.7 25.1 %collective-permute-start.42 = (bf16[512,512]{1,0:T(8,128)(2,1)S(1)}, bf16[512,512]{1,0:T(8,128)(2,1)}, u32[]{:S(2)}, u32[]{:S(2)}) collective-permute-start(bf16[512,512]{1,0:T(8,128)(2,1)S(1)} %collective-permute-done.38.refs_2_), channel_id=1, source_target_pairs={{0,1},{1,0},{2,3},{3,2},{4,5},{5,4},{6,7},{7,6},{8,9},{9,8},{10,11... | collective-permute-start | bytes 1572872 | tf_op jit(solution)/shard_map/ppermute | solution.py:295
  227.2 24.6 %collective-permute-start.43 = (bf16[512,512]{1,0:T(8,128)(2,1)}, bf16[512,512]{1,0:T(8,128)(2,1)}, u32[]{:S(2)}, u32[]{:S(2)}) collective-permute-start(bf16[512,512]{1,0:T(8,128)(2,1)} %collective-permute-done.39.refs_3_), channel_id=1, source_target_pairs={{0,1},{1,0},{2,3},{3,2},{4,5},{5,4},{6,7},{7,6},{8,9},{9,8},{10,11... | collective-permute-start | bytes 1572872 | tf_op jit(solution)/shard_map/ppermute | solution.py:295
  (80 other events, 864.2 us)
Sparse Core Ops, SparseCore 0:
  10.1 128.6 all-gather.2
where the time goes:
time: 318 us; the launch traced here: 313 us
  waiting for transfers between devices  101 us (32%)
  Pallas kernels  86.8 us (27%)
  starting transfers between devices  75.5 us (24%)
  local copies, waits for them, and re-layouts  31.6 us (10%)
  between operations  14.8 us (5%)
  other arithmetic  3.35 us (1%)
    ppermute x24, waiting for transfers between devices, ring(): return [a] + [lax.ppermute(a, axis, pairs(-d)) for d in (1, 2, 3)]  74.9 us
    ppermute x24, starting transfers between devices, ring(): return [a] + [lax.ppermute(a, axis, pairs(-d)) for d in (1, 2, 3)]  46.7 us
    pallas_call x3, Pallas kernels, project(): pl.pallas_call(project_kernel, out_shape=jax.ShapeDtypeStruct((count, row...  27.8 us
    unnamed x126, local copies, waits for them, and re-layouts  27 us
    pallas_call x2, Pallas kernels, medium(): pl.pallas_call(functools.partial(conv_kernel, extra), out_shape=jax.Shape...  22.2 us
    ppermute x1, waiting for transfers between devices, on_device(): rim = lax.ppermute(qkv_first[:, length - HALO:], 'ctx', ahead)  19.4 us
    pallas_call x2, Pallas kernels, collect(): pl.pallas_call(collect_kernel, out_shape=(jax.ShapeDtypeStruct((8, rows,...  13.3 us
    pallas_call x2, Pallas kernels, mix(): pl.pallas_call(mix_kernel, out_shape=jax.ShapeDtypeStruct((rows, channels...  9.66 us
  transfers between devices with their start and end apart: 51, of which 15 were waited for; matrix products, arithmetic and copies ran while one was open for 3% of the time, Pallas kernels for 23%

commit v1 on v0

--- a/solution.py
+++ b/solution.py
@@ -1,6 +1,3 @@
-import functools
-
-
 import jax
 import jax.numpy as jnp
 from jax import lax
@@ -11,7 +8,8 @@
 HALO = 144
 
 
-def conv_kernel(extra, prev_ref, cur_ref, taps_ref, filt_ref, gain_ref, out_ref, k_ref, v_ref, g_ref, d_ref, r_ref, y_ref):
+def conv_kernel(prev_ref, cur_ref, taps_ref, filt_ref, *refs):
+    out_ref, k_ref, v_ref, g_ref, d_ref, r_ref, y_ref = refs[-7:]
     length = cur_ref.shape[1]
     lag = 4 * filt_ref.shape[1]
     block = length // 8
@@ -34,12 +32,18 @@
     def spread(k):
         return g_ref[pl.ds(k, 8, stride=block), :]
 
-    for n in range((block + lag) // 4):
-        e = [spread(4 * n + q) for q in range(4)]
-        for w, (first, second) in enumerate(((e[0], e[2]), (e[1], e[3]), (e[0] + e[1], e[2] + e[3]))):
-            d_ref[3 * w, n] = first
-            d_ref[3 * w + 1, n] = second
-            d_ref[3 * w + 2, n] = first + second
+    def split(step, carry):
+        for n in range(4):
+            n = step * 4 + n
+            e = [spread(4 * n + q) for q in range(4)]
+            pairs = ((e[0], e[2]), (e[1], e[3]), (e[0] + e[1], e[2] + e[3]))
+            for w, (first, second) in enumerate(pairs):
+                d_ref[3 * w, n] = first
+                d_ref[3 * w + 1, n] = second
+                d_ref[3 * w + 2, n] = first + second
+        return carry
+
+    lax.fori_loop(0, (block + lag) // 16, split, 0)
     count = block // 4 + 1
     base = lag // 4 - 1
 
@@ -56,41 +60,47 @@
 
     lax.fori_loop(0, 9, short, 0)
 
-    def joined(w, i):
-        if i % 2:
-            return r_ref[3 * w, i // 2 + 1] + r_ref[3 * w + 1, i // 2]
-        return r_ref[3 * w + 2, i // 2] - r_ref[3 * w, i // 2] - r_ref[3 * w + 1, i // 2]
-
-    late = joined(1, 0)
-    for i in range(block // 2):
-        even, odd, both = (joined(w, i + 1) for w in range(3))
-        y_ref[pl.ds(2 * i, 8, stride=block), :] = even + late
-        y_ref[pl.ds(2 * i + 1, 8, stride=block), :] = both - even - odd
-        late = odd
+    def before(w, m):
+        return r_ref[3 * w + 2, m] - r_ref[3 * w, m] - r_ref[3 * w + 1, m]
+
+    def exact(w, m):
+        return r_ref[3 * w, m + 1] + r_ref[3 * w + 1, m]
+
+    def join(step, late):
+        for n in range(2):
+            m = step * 2 + n
+            for k, part in enumerate((exact, before)):
+                even, odd, both = (part(w, m + k) for w in range(3))
+                at = 4 * m + 2 * k
+                y_ref[pl.ds(at, 8, stride=block), :] = even + late
+                y_ref[pl.ds(at + 1, 8, stride=block), :] = both - even - odd
+                late = odd
+        return late
+
+    lax.fori_loop(0, block // 8, join, before(1, 0))
     k_ref[:keep, :] = prev_ref[0, prev_ref.shape[1] - keep :, :].astype(jnp.float32)
     k_ref[keep:, :] = cur_ref[0].astype(jnp.float32)
     for r in range(0, length, 128):
         query = feature(k_ref, 0, keep + r, 128)
         out_ref[r : r + 128, :] = (query * y_ref[r : r + 128, :]).astype(jnp.bfloat16)
-    if extra:
-        out_ref[length:, :] = jnp.broadcast_to(gain_ref[...], (extra, 128))
-
-
-def medium(prev, prev_rows, prev_at, qkv, at, taps, filt, gain, extra):
+
+
+def medium(prev, prev_rows, prev_at, qkv, at, taps, filt, groups, start=0, onto=()):
     length, channels = ROWS, qkv.shape[2]
     lag = 4 * filt.shape[1]
     return pl.pallas_call(
-        functools.partial(conv_kernel, extra),
-        out_shape=jax.ShapeDtypeStruct((length + extra, channels), jnp.bfloat16),
-        grid=(channels // 128,),
+        conv_kernel,
+        out_shape=jax.ShapeDtypeStruct((length, channels), jnp.bfloat16),
+        grid=(groups,),
         in_specs=[
-            pl.BlockSpec((3, prev_rows, 128), lambda g: (0, prev_at, g)),
-            pl.BlockSpec((3, length, 128), lambda g: (0, at, g)),
-            pl.BlockSpec((3, 3, 128), lambda g: (0, 0, g)),
-            pl.BlockSpec((9, lag // 4, 128), lambda g: (0, 0, g)),
-            pl.BlockSpec((1, 128), lambda g: (0, g)),
-        ],
-        out_specs=pl.BlockSpec((length + extra, 128), lambda g: (0, g)),
+            pl.BlockSpec((3, prev_rows, 128), lambda g: (0, prev_at, g + start)),
+            pl.BlockSpec((3, length, 128), lambda g: (0, at, g + start)),
+            pl.BlockSpec((3, 3, 128), lambda g: (0, 0, g + start)),
+            pl.BlockSpec((9, lag // 4, 128), lambda g: (0, 0, g + start)),
+        ]
+        + [pl.BlockSpec(memory_space=pl.ANY)] * len(onto),
+        out_specs=pl.BlockSpec((length, 128), lambda g: (0, g + start)),
+        input_output_aliases={4: 0} if onto else {},
         scratch_shapes=[
             pltpu.VMEM((length + lag + 8, 128), jnp.float32),
             pltpu.VMEM((length + lag + 8, 128), jnp.float32),
@@ -101,7 +111,7 @@
         ],
         compiler_params=pltpu.CompilerParams(vmem_limit_bytes=16 << 20),
         name="medium",
-    )(prev, qkv, taps, filt, gain.reshape(1, channels))
+    )(prev, qkv, taps, filt, *onto)
 
 
 def split_taps(filters):
@@ -134,8 +144,8 @@
     poles = rates_ref.shape[0]
     length = 2 * lower_ref.shape[1]
     block = length // 8
-    kf = featurize_into(edge_ref, lower_ref, upper_ref, 1, 0, taps_ref, 1, k_ref)
-    vf = featurize_into(edge_ref, lower_ref, upper_ref, 2, 1, taps_ref, 2, v_ref)
+    kf = featurize_into(edge_ref, lower_ref, upper_ref, 0, 0, taps_ref, 1, k_ref)
+    vf = featurize_into(edge_ref, lower_ref, upper_ref, 1, 1, taps_ref, 2, v_ref)
     for r in range(0, length, 128):
         gated = (kf(r, 128) * vf(r, 128)).astype(jnp.bfloat16)
         g_ref[r : r + 128, :] = gated.astype(jnp.float32)
@@ -177,9 +187,9 @@
         ),
         grid=(channels // 128,),
         in_specs=[
-            pl.BlockSpec((3, 16, 128), lambda g: (0, 0, g)),
+            pl.BlockSpec((2, 16, 128), lambda g: (0, 0, g)),
             pl.BlockSpec((2, half, 128), lambda g: (0, 0, g)),
-            pl.BlockSpec((3, half, 128), lambda g: (0, 0, g)),
+            pl.BlockSpec((2, half, 128), lambda g: (0, 0, g)),
             pl.BlockSpec((3, 3, 128), lambda g: (0, 0, g)),
             line(poles),
         ],
@@ -262,6 +272,7 @@
 D = 4096
 EPSILON = 1e-05
 ROWS = 512
+HALF = 256
 EXTRA = 16
 
 
@@ -290,21 +301,31 @@
     return ring(jnp.stack(pieces), "ctx", second)
 
 
-def token_gather(a):
+def near_gather(a):
     pieces = ring(a, "tp", z_pairs)
     return (*pieces, *[lax.ppermute(p, "tp", core_pairs()) for p in pieces])
 
 
+def token_gather(a):
+    after = lax.ppermute(a, "tp", z_pairs(-1))
+    before = lax.ppermute(a, "tp", z_pairs(1))
+    low = lax.ppermute(after[:HALF], "tp", z_pairs(-1))
+    high = lax.ppermute(before[HALF:], "tp", z_pairs(1))
+    pieces = (a, after, low, high, before)
+    return (*pieces, *[lax.ppermute(p, "tp", core_pairs()) for p in pieces])
+
+
 def mix_kernel(place_ref, *refs):
     acts, west, south, refs = refs[:8], refs[8:12], refs[12:16], refs[16:]
-    residual_ref, out_ref, act_ref = refs
+    residual_ref, gain_ref, out_ref, send_ref, act_ref = refs
     y, x, z, core = (place_ref[n] for n in range(4))
     rows = act_ref.shape[1]
     for s in range(2):
         for dz in range(4):
             at = (z + dz) % 4 * 4 + (core ^ s) * 2
             for h in range(2):
-                act_ref[at + h] = acts[4 * s + dz][:rows, h * 256 : h * 256 + 256]
+                act_ref[at + h] = acts[4 * s + dz][:, h * 256 : h * 256 + 256]
+    squares = jnp.zeros((EXTRA, rows), jnp.float32)
     for side, weights in enumerate((west, south)):
         total = jnp.zeros((rows, 256), jnp.float32)
         for outer in range(4):
@@ -319,89 +340,104 @@
                 preferred_element_type=jnp.float32,
             )
         lanes = slice(side * 256, side * 256 + 256)
-        wide = residual_ref[:, lanes].astype(jnp.float32)
-        out_ref[:, lanes] = (wide + total).astype(jnp.bfloat16)
-
-
-def mix(place, acts, west, south, residual, at):
+        hidden = (residual_ref[:, lanes].astype(jnp.float32) + total).astype(jnp.bfloat16)
+        out_ref[:, lanes] = hidden
+        wide = hidden.astype(jnp.float32)
+        gain = gain_ref[:, lanes].astype(jnp.float32)
+        send_ref[:rows, lanes] = (wide * gain).astype(jnp.bfloat16)
+        squares = squares + lax.dot_general(
+            jnp.ones((EXTRA, 256), jnp.float32),
+            wide * wide,
+            (((1,), (1,)), ((), ())),
+            precision=lax.Precision.HIGHEST,
+            preferred_element_type=jnp.float32,
+        )
+    high = squares.astype(jnp.bfloat16)
+    rest = squares - high.astype(jnp.float32)
+    middle = rest.astype(jnp.bfloat16)
+    low = (rest - middle.astype(jnp.float32)).astype(jnp.bfloat16)
+    row = lax.broadcasted_iota(jnp.int32, squares.shape, 0)
+    terms = [a.astype(jnp.float32) for a in (high, middle, low)]
+    terms = jnp.where(row == 0, terms[0], jnp.where(row == 1, terms[1], terms[2]))
+    send_ref[rows:, :] = terms.astype(jnp.bfloat16)
+
+
+def mix(place, acts, west, south, residual, gain, at):
     rows, channels = ROWS, acts[0].shape[1]
     whole = lambda a: pl.BlockSpec(a.shape, lambda j, _: (0,) * a.ndim)
     return pl.pallas_call(
         mix_kernel,
-        out_shape=jax.ShapeDtypeStruct((rows, channels), jnp.bfloat16),
+        out_shape=(
+            jax.ShapeDtypeStruct((rows, channels), jnp.bfloat16),
+            jax.ShapeDtypeStruct((rows + EXTRA, channels), jnp.bfloat16),
+        ),
         grid_spec=pltpu.PrefetchScalarGridSpec(
             num_scalar_prefetch=1,
             grid=(1,),
             in_specs=[whole(a) for a in (*acts, *west, *south)]
-            + [pl.BlockSpec((rows, channels), lambda j, _: (at, 0))],
-            out_specs=pl.BlockSpec((rows, channels), lambda j, _: (0, 0)),
+            + [
+                pl.BlockSpec((rows, channels), lambda j, _: (at, 0)),
+                pl.BlockSpec((1, channels), lambda j, _: (0, 0)),
+            ],
+            out_specs=(
+                pl.BlockSpec((rows, channels), lambda j, _: (0, 0)),
+                pl.BlockSpec((rows + EXTRA, channels), lambda j, _: (0, 0)),
+            ),
             scratch_shapes=[pltpu.VMEM((16, rows, 256), jnp.bfloat16)],
         ),
         compiler_params=pltpu.CompilerParams(vmem_limit_bytes=40 << 20),
         name="mix",
-    )(place, *acts, *west, *south, residual)
-
-
-def collect_kernel(place_ref, *refs):
-    acts, gains, (act_ref, scale_ref) = refs[:8], refs[8:16], refs[16:]
+    )(place, *acts, *west, *south, residual, gain.reshape(1, channels))
+
+
+def project_kernel(place_ref, *refs):
+    acts, (weight_ref, out_ref, scale_ref) = refs[:10], refs[10:]
     z, core = place_ref[2], place_ref[3]
-    squares = jnp.zeros(scale_ref.shape, jnp.float32)
+    rows = out_ref.shape[1]
+
+    @pl.when((pl.program_id(0) == 0) & (pl.program_id(1) == 0))
+    def _():
+        total = jnp.zeros((1, rows), jnp.float32)
+        for ref in acts[:2] + acts[3:7] + acts[8:]:
+            terms = ref[ref.shape[0] - EXTRA :, :].astype(jnp.float32)
+            total = total + (terms[0:1, :] + terms[1:2, :] + terms[2:3, :])
+        scale = lax.rsqrt(total / D + EPSILON)
+        scale_ref[...] = jnp.transpose(jnp.broadcast_to(scale, (128, rows)))
+
+    left, right = [], []
     for s in range(2):
         for dz in range(4):
-            wide = acts[4 * s + dz][...].astype(jnp.float32)
-            gain = gains[4 * s + dz][:1, :].astype(jnp.float32)
-            act_ref[(z + dz) % 4 * 2 + (core ^ s)] = (wide * gain).astype(jnp.bfloat16)
-            wide = wide * wide
-            for n in range(0, wide.shape[1], 128):
-                squares = squares + wide[:, n : n + 128]
-    total = jnp.sum(squares, axis=1, keepdims=True)
-    scale_ref[...] = jnp.broadcast_to(lax.rsqrt(total / D + EPSILON), squares.shape)
-
-
-def collect(place, acts, gains):
-    rows, channels = acts[0].shape
-    return pl.pallas_call(
-        collect_kernel,
-        out_shape=(
-            jax.ShapeDtypeStruct((8, rows, channels), jnp.bfloat16),
-            jax.ShapeDtypeStruct((rows, 128), jnp.float32),
-        ),
-        grid_spec=pltpu.PrefetchScalarGridSpec(
-            num_scalar_prefetch=1,
-            grid=(1,),
-            in_specs=[pl.BlockSpec((rows, channels), lambda j, _: (0, 0)) for a in acts]
-            + [pl.BlockSpec((EXTRA, channels), lambda j, _: (ROWS // EXTRA, 0)) for a in gains],
-            out_specs=(
-                pl.BlockSpec((8, rows, channels), lambda j, _: (0, 0, 0)),
-                pl.BlockSpec((rows, 128), lambda j, _: (0, 0)),
-            ),
-        ),
-        name="collect",
-    )(place, *acts, *gains)
-
-
-def project_kernel(act_ref, scale_ref, weight_ref, out_ref):
-    left = jnp.concatenate([act_ref[n] for n in range(8)], axis=1)
-    right = jnp.concatenate([weight_ref[n, 0] for n in range(16)], axis=0)
-    total = jnp.dot(left, right, preferred_element_type=jnp.float32)
+            if dz == 2:
+                parts = [acts[5 * s + 2][...], acts[5 * s + 3][:HALF, :]]
+                left.append(jnp.concatenate(parts, axis=0))
+            else:
+                left.append(acts[5 * s + (0, 1, 2, 4)[dz]][:rows, :])
+            at = (z + dz) % 4 * 4 + (core ^ s) * 2
+            right += [weight_ref[at, 0], weight_ref[at + 1, 0]]
+    total = jnp.dot(
+        jnp.concatenate(left, axis=1),
+        jnp.concatenate(right, axis=0),
+        preferred_element_type=jnp.float32,
+    )
     scale = jnp.concatenate([scale_ref[...], scale_ref[...]], axis=1)
     out_ref[0] = (total * scale).astype(jnp.bfloat16)
 
 
-def project(act, scale, weight, start, count):
-    blocks, rows, channels = act.shape
+def project(place, acts, weight, start, count):
+    rows, channels = ROWS, acts[0].shape[1]
     return pl.pallas_call(
         project_kernel,
         out_shape=jax.ShapeDtypeStruct((count, rows, channels), jnp.bfloat16),
-        grid=(count, channels // 256),
-        in_specs=[
-            pl.BlockSpec((blocks, rows, channels), lambda m, n: (0, 0, 0)),
-            pl.BlockSpec((rows, 128), lambda m, n: (0, 0)),
-            pl.BlockSpec((16, 1, 256, 256), lambda m, n: (0, m + start, 0, n)),
-        ],
-        out_specs=pl.BlockSpec((1, rows, 256), lambda m, n: (m, 0, n)),
+        grid_spec=pltpu.PrefetchScalarGridSpec(
+            num_scalar_prefetch=1,
+            grid=(count, channels // 256),
+            in_specs=[pl.BlockSpec(a.shape, lambda m, n, _: (0, 0)) for a in acts]
+            + [pl.BlockSpec((16, 1, 256, 256), lambda m, n, _: (0, m + start, 0, n))],
+            out_specs=pl.BlockSpec((1, rows, 256), lambda m, n, _: (m, 0, n)),
+            scratch_shapes=[pltpu.VMEM((rows, 128), jnp.float32)],
+        ),
         name="project",
-    )(act, scale, weight)
+    )(place, *acts, weight)
 
 
 def on_device(
@@ -424,8 +460,6 @@
     place = jnp.stack([y, x, z, core]).astype(jnp.int32)
     ahead = [(i, i + 1) for i in range(15)]
 
-    rim = lax.ppermute(qkv_first[:, length - HALO :], "ctx", ahead)
-
     packed = out_weight.reshape(2, 256, 256)
     odd = c % 2
     turned = []
@@ -437,34 +471,39 @@
                 pairs.append((cc * 8 + tt, to[0] * 8 + to[1]))
         mine = lax.dynamic_index_in_dim(packed, (odd + k) % 2, 0, False)
         turned.append(lax.ppermute(mine, ("ctx", "tp"), pairs))
+    rim = lax.ppermute(qkv_first[:, length - HALO :], "ctx", ahead)
     first = jnp.where(odd == 0, turned[0], turned[1])
     second = jnp.where(odd == 0, turned[1], turned[0])
-    weight = lax.all_gather(in_weight, "ctx")
+    weight = lax.all_gather(in_weight[1:], "ctx")
+    query_weight = lax.all_gather(in_weight[:1], "ctx")
     out_west = plane_gather(first, x_pairs, y_pairs)
     out_south = plane_gather(second, y_pairs, x_pairs)
 
     filt = split_taps(medium_filter)
-    upper = medium(qkv_first, 256, 1, qkv_first, 1, short_first, filt, norm_gain, EXTRA)
-    upper_pieces = token_gather(upper)
-    lower = medium(rim, HALO, 0, qkv_first, 0, short_first, filt, norm_gain, 0)
-    lower_pieces = token_gather(lower)
-    hidden_upper = mix(place, upper_pieces, out_west, out_south, residual_in, 1)
-    hidden_upper_pieces = token_gather(hidden_upper)
-    hidden_lower = mix(place, lower_pieces, out_west, out_south, residual_in, 0)
-    hidden_lower_pieces = token_gather(hidden_lower)
+    upper = medium(qkv_first, 256, 1, qkv_first, 1, short_first, filt, 2)
+    upper = medium(qkv_first, 256, 1, qkv_first, 1, short_first, filt, 2, 2, (upper,))
+    upper_pieces = near_gather(upper)
+    lower = medium(rim, HALO, 0, qkv_first, 0, short_first, filt, 4)
+    lower_pieces = near_gather(lower)
+    hidden_upper, send_upper = mix(
+        place, upper_pieces, out_west, out_south, residual_in, norm_gain, 1
+    )
+    send_upper = token_gather(send_upper)
+    hidden_lower, send_lower = mix(
+        place, lower_pieces, out_west, out_south, residual_in, norm_gain, 0
+    )
+    send_lower = token_gather(send_lower)
     hidden = jnp.concatenate([hidden_lower, hidden_upper], axis=0)
-    act, scale = collect(place, hidden_upper_pieces, upper_pieces)
-    qkv_upper = project(act, scale, weight, 0, 3)
-    edge = lax.ppermute(qkv_upper[:, ROWS - 16 :], "ctx", ahead)
-    act, scale = collect(place, hidden_lower_pieces, upper_pieces)
-    kv_lower = project(act, scale, weight, 1, 2)
-    u, starts, end = modal_scan(edge, kv_lower, qkv_upper, short_second, rates)
+    kv_upper = project(place, send_upper, weight, 0, 2)
+    edge = lax.ppermute(kv_upper[:, ROWS - 16 :], "ctx", ahead)
+    kv_lower = project(place, send_lower, weight, 0, 2)
+    u, starts, end = modal_scan(edge, kv_lower, kv_upper, short_second, rates)
     log_decay = -rates * length
 
     def decay(k):
         return jnp.exp(log_decay * k.astype(jnp.float32))
 
-    along = [end] + [lax.ppermute(end, "ctx", x_pairs(-d)) for d in (1, 2, 3)]
+    along = ring(end, "ctx", x_pairs)
     row = jnp.zeros_like(rates)
     enter = jnp.zeros_like(rates)
     for d, e in enumerate(along):
@@ -473,15 +512,18 @@
         row = row + decay(3 - at) * wide
         enter = enter + jnp.where(at < x, decay(jnp.maximum(x - 1 - at, 0)), 0.0) * wide
     row = row.astype(jnp.bfloat16)
+    up = ring(row, "ctx", y_pairs)
     for d in (1, 2, 3):
-        e = lax.ppermute(row, "ctx", y_pairs(-d))
+        e = up[d]
         at = (y + d) % 4
         enter = enter + jnp.where(
             at < y, decay(x + 4 * jnp.maximum(y - 1 - at, 0)), 0.0
         ) * e.astype(jnp.float32)
-    q_lower = project(act, scale, weight, 0, 1)
+    q_upper = project(place, send_upper, query_weight, 0, 1)
+    edge = lax.ppermute(q_upper[:, ROWS - 16 :], "ctx", ahead)
+    q_lower = project(place, send_lower, query_weight, 0, 1)
     mixed = modal_finish(
-        edge, q_lower, qkv_upper, short_second, rates, residues, skip_gain, u, starts, enter
+        edge, q_lower, q_upper, short_second, rates, residues, skip_gain, u, starts, enter
     )
     return (hidden, mixed)
 

time: 318 us -> 301 us (0.947)
  waiting for transfers between devices: 101 us -> 77.1 us
  starting transfers between devices: 75.5 us -> 82.5 us
  Pallas kernels: 86.8 us -> 81.8 us
    ppermute x24, waiting for transfers between devices: 74.9 us -> 44.2 us  [ring(): return [a] + [lax.ppermute(a, axis, pairs(-d)) for d in (1, 2, 3)]]
    ppermute x7 -> x18, waiting for transfers between devices: 1.8 us -> 27.4 us  [the longest x2 13 us: token_gather(): low = lax.ppermute(after[:HALF], 'tp', z_pairs(-1))]
    ppermute x1, waiting for transfers between devices: 19.4 us -> 0.01 us  [on_device(): rim = lax.ppermute(qkv_first[:, length - HALO:], 'ctx', ahead)]
    pallas_call x6 -> x5, Pallas kernels: 45.1 us -> 34.1 us  [the longest x3 23.2 us: medium(): pl.pallas_call(conv_kernel, out_shape=jax.ShapeDtypeStruct((length, chann...]
    ppermute x7 -> x18, starting transfers between devices: 13.8 us -> 20.4 us  [the longest x2 6.97 us: token_gather(): low = lax.ppermute(after[:HALF], 'tp', z_pairs(-1))]
    pallas_call x3 -> x4, Pallas kernels: 27.8 us -> 34 us  [project(): pl.pallas_call(project_kernel, out_shape=jax.ShapeDtypeStruct((count, row...]
    slice x1 -> x8, local copies, waits for them, and re-layouts: 0.8 us -> 6.1 us  [the longest x1 1.9 us: on_device(): weight = lax.all_gather(in_weight[1:], 'ctx')]
    unnamed x126 -> x130, local copies, waits for them, and re-layouts: 27 us -> 25.5 us
  transfers between devices with their start and end apart: 51 -> 57, of which waited for: 15 -> 18; matrix products, arithmetic and copies ran while one was open for 3% -> 4% of each run, Pallas kernels for 23% -> 25%
where the time goes in v1:
time: 301 us; the launch traced here: 295 us
  starting transfers between devices  82.5 us (27%)
  Pallas kernels  81.8 us (27%)
  waiting for transfers between devices  77.1 us (26%)
  local copies, waits for them, and re-layouts  34.4 us (11%)
  between operations  14.8 us (5%)
  other arithmetic  4.57 us (2%)
    ppermute x24, starting transfers between devices, ring(): return [a] + [lax.ppermute(a, axis, pairs(-d)) for d in (1, 2, 3)]  49.3 us
    ppermute x24, waiting for transfers between devices, ring(): return [a] + [lax.ppermute(a, axis, pairs(-d)) for d in (1, 2, 3)]  44.2 us
    pallas_call x4, Pallas kernels, project(): pl.pallas_call(project_kernel, out_shape=jax.ShapeDtypeStruct((count, row...  34 us
    unnamed x130, local copies, waits for them, and re-layouts  25.5 us
    pallas_call x3, Pallas kernels, medium(): pl.pallas_call(conv_kernel, out_shape=jax.ShapeDtypeStruct((length, chann...  23.2 us
    ppermute x2, waiting for transfers between devices, token_gather(): low = lax.ppermute(after[:HALF], 'tp', z_pairs(-1))  13 us
    ppermute x2, waiting for transfers between devices, token_gather(): high = lax.ppermute(before[HALF:], 'tp', z_pairs(1))  12 us
    pallas_call x2, Pallas kernels, mix(): pl.pallas_call(mix_kernel, out_shape=(jax.ShapeDtypeStruct((rows, channel...  10.9 us
  transfers between devices with their start and end apart: 57, of which 18 were waited for; matrix products, arithmetic and copies ran while one was open for 4% of the time, Pallas kernels for 25%

profile of v1, /device:TPU:28, one launch (start us, length us, event | category | flops | bytes accessed | tf_op | source)
XLA Modules:
  0.0 295.2 jit_solution(16672149237226172367)
XLA Ops:
  11.7 3.1 %collective-permute-start.9 = (bf16[256,256]{1,0:T(8,128)(2,1)}, bf16[256,256]{1,0:T(8,128)(2,1)}, u32[]{:S(2)}, u32[]{:S(2)}) collective-permute-start(bf16[256,256]{1,0:T(8,128)(2,1)} %get-tuple-element.18), channel_id=1, source_target_pairs={{0,8},{1,24},{2,40},{3,56},{4,72},{5,88},{6,104},{7,120},{8,0},{9,... | collective-permute-start | bytes 393224 | tf_op jit(solution)/shard_map/ppermute | solution.py:473
  14.8 6.0 %collective-permute-start.8 = (bf16[256,256]{1,0:T(8,128)(2,1)}, bf16[256,256]{1,0:T(8,128)(2,1)}, u32[]{:S(2)}, u32[]{:S(2)}) collective-permute-start(bf16[256,256]{1,0:T(8,128)(2,1)} %get-tuple-element.19), channel_id=1, source_target_pairs={{0,0},{1,16},{2,32},{3,48},{4,64},{5,80},{6,96},{7,112},{8,8},{9,2... | collective-permute-start | bytes 393224 | tf_op jit(solution)/shard_map/ppermute | solution.py:473
  24.0 4.6 %collective-permute-done.8 = bf16[256,256]{1,0:T(8,128)(2,1)} collective-permute-done((bf16[256,256]{1,0:T(8,128)(2,1)}, bf16[256,256]{1,0:T(8,128)(2,1)}, u32[]{:S(2)}, u32[]{:S(2)}) %collective-permute-start.8) | collective-permute-done | bytes 131104 | tf_op jit(solution)/shard_map/ppermute | solution.py:473
  30.0 4.0 %collective-permute-start.11 = (bf16[256,256]{1,0:T(8,128)(2,1)S(1)}, bf16[256,256]{1,0:T(8,128)(2,1)S(1)}, u32[]{:S(2)}, u32[]{:S(2)}) collective-permute-start(bf16[256,256]{1,0:T(8,128)(2,1)S(1)} %get-tuple-element.17), channel_id=1, source_target_pairs={{0,16},{8,24},{16,0},{24,8},{32,48},{40,56},{48,32},{56,40},{64,80... | collective-permute-start | bytes 393224 | tf_op jit(solution)/shard_map/ppermute | solution.py:296
  34.1 5.7 %medium.4.refs_0_ = bf16[512,512]{1,0:T(8,128)(2,1)S(1)} custom-call(bf16[3,1024,512]{2,1,0:T(8,128)(2,1)S(1)} %copy-done, bf16[3,1024,512]{2,1,0:T(8,128)(2,1)S(1)} %copy-done, f32[3,3,512]{2,1,0:T(4,128)S(1)} %copy-done.46, f32[9,32,512]{2,1,0:T(8,128)S(1)} %add_dynamic-update-slice_fusion.filt_ref), custom_call_target="tpu_custom_call" | custom-call | tf_op jit(solution)/shard_map/medium/pallas_call | solution.py:91
  39.7 5.7 %medium.5.refs_0_ = bf16[512,512]{1,0:T(8,128)(2,1)S(1)} custom-call(bf16[3,1024,512]{2,1,0:T(8,128)(2,1)S(1)} %copy-done, bf16[3,1024,512]{2,1,0:T(8,128)(2,1)S(1)} %copy-done, f32[3,3,512]{2,1,0:T(4,128)S(1)} %copy-done.46, f32[9,32,512]{2,1,0:T(8,128)S(1)} %add_dynamic-update-slice_fusion.filt_ref, ...), custom_call_target="tpu_custom_call", output_to_operand_aliasing={{}: (4, {})} | custom-call | tf_op jit(solution)/shard_map/medium/pallas_call | solution.py:91
  49.6 6.3 %collective-permute-start.18 = (bf16[256,256]{1,0:T(8,128)(2,1)S(1)}, bf16[256,256]{1,0:T(8,128)(2,1)S(1)}, u32[]{:S(2)}, u32[]{:S(2)}) collective-permute-start(bf16[256,256]{1,0:T(8,128)(2,1)S(1)} %get-tuple-element.16), channel_id=1, source_target_pairs={{0,32},{8,40},{16,48},{24,56},{32,64},{40,72},{48,80},{56,88},{64,... | collective-permute-start | bytes 393224 | tf_op jit(solution)/shard_map/ppermute | solution.py:296
  56.0 6.8 %collective-permute-done.18 = bf16[256,256]{1,0:T(8,128)(2,1)S(1)} collective-permute-done((bf16[256,256]{1,0:T(8,128)(2,1)S(1)}, bf16[256,256]{1,0:T(8,128)(2,1)S(1)}, u32[]{:S(2)}, u32[]{:S(2)}) %collective-permute-start.18) | collective-permute-done | bytes 131104 | tf_op jit(solution)/shard_map/ppermute | solution.py:296
  62.8 2.9 collective-permute-done.17
  65.7 3.0 %collective-permute-start.16 = (bf16[256,256]{1,0:T(8,128)(2,1)S(1)}, bf16[256,256]{1,0:T(8,128)(2,1)S(1)}, u32[]{:S(2)}, u32[]{:S(2)}) collective-permute-start(bf16[256,256]{1,0:T(8,128)(2,1)S(1)} %get-tuple-element.16), channel_id=1, source_target_pairs={{0,96},{8,104},{16,112},{24,120},{32,0},{40,8},{48,16},{56,24},{64... | collective-permute-start | bytes 393224 | tf_op jit(solution)/shard_map/ppermute | solution.py:296
  68.8 7.4 %collective-permute-done.16 = bf16[256,256]{1,0:T(8,128)(2,1)S(1)} collective-permute-done((bf16[256,256]{1,0:T(8,128)(2,1)S(1)}, bf16[256,256]{1,0:T(8,128)(2,1)S(1)}, u32[]{:S(2)}, u32[]{:S(2)}) %collective-permute-start.16) | collective-permute-done | bytes 131104 | tf_op jit(solution)/shard_map/ppermute | solution.py:296
  82.5 9.6 %collective-permute-start.20 = (bf16[4,256,256]{2,1,0:T(8,128)(2,1)S(1)}, bf16[4,256,256]{2,1,0:T(8,128)(2,1)S(1)}, u32[]{:S(2)}, u32[]{:S(2)}) collective-permute-start(bf16[4,256,256]{2,1,0:T(8,128)(2,1)S(1)} %pad_maximum_fusion.2.refs_12_), channel_id=1, source_target_pairs={{0,16},{8,24},{16,0},{24,8},{32,48},{40,56},{48,32},{56,40},{64,80... | collective-permute-start | bytes 1572872 | tf_op jit(solution)/shard_map/ppermute | solution.py:296
  92.1 11.9 %medium.3.refs_0_ = bf16[512,512]{1,0:T(8,128)(2,1)} custom-call(bf16[3,144,512]{2,1,0:T(8,128)(2,1)S(1)} %collective-permute-done.prev_ref, bf16[3,1024,512]{2,1,0:T(8,128)(2,1)S(1)} %copy-done, f32[3,3,512]{2,1,0:T(4,128)S(1)} %copy-done.46, f32[9,32,512]{2,1,0:T(8,128)S(1)} %add_dynamic-update-slice_fusion.filt_ref), custom_call_target="tpu_custom_call" | custom-call | tf_op jit(solution)/shard_map/medium/pallas_call | solution.py:91
  107.3 5.8 %collective-permute-done.14.refs_10_ = bf16[4,256,256]{2,1,0:T(8,128)(2,1)S(1)} collective-permute-done((bf16[4,256,256]{2,1,0:T(8,128)(2,1)S(1)}, bf16[4,256,256]{2,1,0:T(8,128)(2,1)S(1)}, u32[]{:S(2)}, u32[]{:S(2)}) %collective-permute-start.14) | collective-permute-done | bytes 524320 | tf_op jit(solution)/shard_map/ppermute | solution.py:296
  113.9 2.9 collective-permute-start.1
  120.5 19.3 %collective-permute-done.1.refs_1_ = bf16[512,512]{1,0:T(8,128)(2,1)S(1)} collective-permute-done((bf16[512,512]{1,0:T(8,128)(2,1)}, bf16[512,512]{1,0:T(8,128)(2,1)S(1)}, u32[]{:S(2)}, u32[]{:S(2)}) %collective-permute-start.1) | collective-permute-done | bytes 524320 | tf_op jit(solution)/shard_map/ppermute | solution.py:296
  156.9 5.7 %mix.3 = (bf16[512,512]{1,0:T(8,128)(2,1)S(1)}, bf16[528,512]{1,0:T(8,128)(2,1)S(1)}) custom-call(s32[4]{0:T(128)S(1)} %pad_add_fusion.place_ref, bf16[512,512]{1,0:T(8,128)(2,1)S(1)} %copy-done.2, bf16[512,512]{1,0:T(8,128)(2,1)S(1)} %copy-done.35, bf16[512,512]{1,0:T(8,128)(2,1)S(1)} %copy-done.37, bf16[512,512]{1,0:T(8,128)(2,1)} %collective-permute-done.24.refs_3_, ...), custom_call_target="tpu_custom_call" | custom-call | tf_op jit(solution)/shard_map/mix/pallas_call | solution.py:368
  162.7 3.7 %collective-permute-start.29 = (bf16[528,512]{1,0:T(8,128)(2,1)S(1)}, bf16[528,512]{1,0:T(8,128)(2,1)S(1)}, u32[]{:S(2)}, u32[]{:S(2)}) collective-permute-start(bf16[528,512]{1,0:T(8,128)(2,1)S(1)} %get-tuple-element.11.refs_0_), channel_id=1, source_target_pairs={{0,6},{1,7},{2,0},{3,1},{4,2},{5,3},{6,4},{7,5},{8,14},{9,15},{10,... | collective-permute-start | bytes 1622024 | tf_op jit(solution)/shard_map/ppermute | solution.py:310
  170.1 5.2 %mix.2 = (bf16[512,512]{1,0:T(8,128)(2,1)S(1)}, bf16[528,512]{1,0:T(8,128)(2,1)S(1)}) custom-call(s32[4]{0:T(128)S(1)} %pad_add_fusion.place_ref, bf16[512,512]{1,0:T(8,128)(2,1)} %medium.3.refs_0_, bf16[512,512]{1,0:T(8,128)(2,1)S(1)} %collective-permute-done.1.refs_1_, bf16[512,512]{1,0:T(8,128)(2,1)S(1)} %collective-permute-done.2.refs_2_, ...), custom_call_target="tpu_custom_call" | custom-call | tf_op jit(solution)/shard_map/mix/pallas_call | solution.py:368
  178.3 3.8 %collective-permute-start.30 = (bf16[256,512]{1,0:T(8,128)(2,1)S(1)}, bf16[256,512]{1,0:T(8,128)(2,1)S(1)}, u32[]{:S(2)}, u32[]{:S(2)}) collective-permute-start(bf16[256,512]{1,0:T(8,128)(2,1)S(1)} %slice.60), channel_id=1, source_target_pairs={{0,6},{1,7},{2,0},{3,1},{4,2},{5,3},{6,4},{7,5},{8,14},{9,15},{10,... | collective-permute-start | bytes 786440 | tf_op jit(solution)/shard_map/ppermute | solution.py:312
  183.1 12.2 %collective-permute-done.30.refs_2_ = bf16[256,512]{1,0:T(8,128)(2,1)S(1)} collective-permute-done((bf16[256,512]{1,0:T(8,128)(2,1)S(1)}, bf16[256,512]{1,0:T(8,128)(2,1)S(1)}, u32[]{:S(2)}, u32[]{:S(2)}) %collective-permute-start.30) | collective-permute-done | bytes 262176 | tf_op jit(solution)/shard_map/ppermute | solution.py:312
  195.4 6.9 %collective-permute-done.32.refs_3_ = bf16[272,512]{1,0:T(8,128)(2,1)S(1)} collective-permute-done((bf16[272,512]{1,0:T(8,128)(2,1)S(1)}, bf16[272,512]{1,0:T(8,128)(2,1)S(1)}, u32[]{:S(2)}, u32[]{:S(2)}) %collective-permute-start.32) | collective-permute-done | bytes 278560 | tf_op jit(solution)/shard_map/ppermute | solution.py:313
  205.5 3.2 %collective-permute-start.40 = (bf16[256,512]{1,0:T(8,128)(2,1)S(1)}, bf16[256,512]{1,0:T(8,128)(2,1)}, u32[]{:S(2)}, u32[]{:S(2)}) collective-permute-start(bf16[256,512]{1,0:T(8,128)(2,1)S(1)} %slice.63), channel_id=1, source_target_pairs={{0,6},{1,7},{2,0},{3,1},{4,2},{5,3},{6,4},{7,5},{8,14},{9,15},{10,... | collective-permute-start | bytes 786440 | tf_op jit(solution)/shard_map/ppermute | solution.py:312
  208.7 5.1 %collective-permute-done.42.refs_3_ = bf16[272,512]{1,0:T(8,128)(2,1)} collective-permute-done((bf16[272,512]{1,0:T(8,128)(2,1)S(1)}, bf16[272,512]{1,0:T(8,128)(2,1)}, u32[]{:S(2)}, u32[]{:S(2)}) %collective-permute-start.42) | collective-permute-done | bytes 278560 | tf_op jit(solution)/shard_map/ppermute | solution.py:313
  214.6 10.1 %project.6.upper_ref = bf16[2,512,512]{2,1,0:T(8,128)(2,1)} custom-call(s32[4]{0:T(128)} %copy-done.49, bf16[528,512]{1,0:T(8,128)(2,1)} %copy-done.13, bf16[528,512]{1,0:T(8,128)(2,1)} %copy-done.53, bf16[256,512]{1,0:T(8,128)(2,1)} %copy-done.59, bf16[272,512]{1,0:T(8,128)(2,1)} %copy-done.57, bf16[528,512]{1,0:T(8,128)(2,1)} %copy-done.51, ...), custom_call_target="tpu_custom_call" | custom-call | tf_op jit(solution)/shard_map/project/pallas_call | solution.py:428
  225.4 3.2 %collective-permute-start.48 = (bf16[2,16,512]{2,1,0:T(8,128)(2,1)S(1)}, bf16[2,16,512]{2,1,0:T(8,128)(2,1)S(1)}, u32[]{:S(2)}, u32[]{:S(2)}) collective-permute-start(bf16[2,16,512]{2,1,0:T(8,128)(2,1)S(1)} %slice.65), channel_id=1, source_target_pairs={{0,8},{8,16},{16,24},{24,32},{32,40},{40,48},{48,56},{56,64},{64,7... | collective-permute-start | bytes 98312 | tf_op jit(solution)/shard_map/ppermute | solution.py:498
  228.7 10.1 %project.7.lower_ref = bf16[2,512,512]{2,1,0:T(8,128)(2,1)} custom-call(s32[4]{0:T(128)} %copy-done.49, bf16[528,512]{1,0:T(8,128)(2,1)} %copy-done.14, bf16[528,512]{1,0:T(8,128)(2,1)} %collective-permute-done.39.refs_1_, bf16[256,512]{1,0:T(8,128)(2,1)} %collective-permute-done.40.refs_2_, bf16[272,512]{1,0:T(8,128)(2,1)} %collective-permute-done.42.refs_3_, ...), custom_call_target="tpu_custom_call" | custom-call | tf_op jit(solution)/shard_map/project/pallas_call | solution.py:428
  240.0 6.3 %modal_scan.1 = (f32[128,8,512]{2,1,0:T(8,128)S(1)}, f32[16,8,512]{2,1,0:T(8,128)S(1)}, bf16[16,512]{1,0:T(8,128)(2,1)S(1)}) custom-call(bf16[2,16,512]{2,1,0:T(8,128)(2,1)S(1)} %collective-permute-done.48.edge_ref, bf16[2,512,512]{2,1,0:T(8,128)(2,1)S(1)} %copy-done.10, bf16[2,512,512]{2,1,0:T(8,128)(2,1)S(1)} %copy-done.9, f32[3,3,512]{2,1,0:T(4,128)S(1)} %copy-done.47, ...), custom_call_target="tpu_custom_call" | custom-call | tf_op jit(solution)/shard_map/modal_scan/pallas_call | solution.py:181
  253.1 6.7 %collective-permute-start.54 = (bf16[16,512]{1,0:T(8,128)(2,1)S(1)}, bf16[16,512]{1,0:T(8,128)(2,1)S(1)}, u32[]{:S(2)}, u32[]{:S(2)}) collective-permute-start(bf16[16,512]{1,0:T(8,128)(2,1)S(1)} %fusion.15), channel_id=1, source_target_pairs={{0,32},{8,40},{16,48},{24,56},{32,64},{40,72},{48,80},{56,88},{64,... | collective-permute-start | bytes 49160 | tf_op jit(solution)/shard_map/ppermute | solution.py:296
  262.9 6.9 %project.4.upper_ref = bf16[1,512,512]{2,1,0:T(8,128)(2,1)} custom-call(s32[4]{0:T(128)} %copy-done.49, bf16[528,512]{1,0:T(8,128)(2,1)} %copy-done.13, bf16[528,512]{1,0:T(8,128)(2,1)} %copy-done.53, bf16[256,512]{1,0:T(8,128)(2,1)} %copy-done.59, bf16[272,512]{1,0:T(8,128)(2,1)} %copy-done.57, bf16[528,512]{1,0:T(8,128)(2,1)} %copy-done.51, ...), custom_call_target="tpu_custom_call" | custom-call | tf_op jit(solution)/shard_map/project/pallas_call | solution.py:428
  272.8 6.9 %project.5.lower_ref = bf16[1,512,512]{2,1,0:T(8,128)(2,1)} custom-call(s32[4]{0:T(128)} %copy-done.49, bf16[528,512]{1,0:T(8,128)(2,1)} %copy-done.14, bf16[528,512]{1,0:T(8,128)(2,1)} %collective-permute-done.39.refs_1_, bf16[256,512]{1,0:T(8,128)(2,1)} %collective-permute-done.40.refs_2_, bf16[272,512]{1,0:T(8,128)(2,1)} %collective-permute-done.42.refs_3_, ...), custom_call_target="tpu_custom_call" | custom-call | tf_op jit(solution)/shard_map/project/pallas_call | solution.py:428
  280.9 7.5 %modal_finish.1 = bf16[1024,512]{1,0:T(8,128)(2,1)} custom-call(bf16[1,16,512]{2,1,0:T(8,128)(2,1)S(1)} %collective-permute-done.38.edge_ref, bf16[1,512,512]{2,1,0:T(8,128)(2,1)S(1)} %copy-done.15, bf16[1,512,512]{2,1,0:T(8,128)(2,1)S(1)} %copy-done.12, f32[3,3,512]{2,1,0:T(4,128)S(1)} %copy-done.47, f32[16,512]{1,0:T(8,128)S(1)} %copy-done.31, ...), custom_call_target="tpu_custom_call" | custom-call | tf_op jit(solution)/shard_map/modal_finish/pallas_call | solution.py:246
  (252 shorter events, 72.0 us)
Async XLA Ops:
  7.2 207.4 %all-gather.7.cloned.1.call-start = ((), (), s32[]{:S(2)}) async-start(), calls=%async_computation.1 | async-start | bytes 8912896 | tf_op jit(solution)/shard_map/all_gather | solution.py:477
  9.1 253.8 %all-gather.5.cloned.1.call-start = ((), (), s32[]{:S(2)}) async-start(), calls=%async_computation | async-start | bytes 4456448 | tf_op jit(solution)/shard_map/all_gather | solution.py:478
  29.5 20.0 %collective-permute-start.12 = (bf16[256,256]{1,0:T(8,128)(2,1)S(1)}, bf16[256,256]{1,0:T(8,128)(2,1)S(1)}, u32[]{:S(2)}, u32[]{:S(2)}) collective-permute-start(bf16[256,256]{1,0:T(8,128)(2,1)S(1)} %get-tuple-element.17), channel_id=1, source_target_pairs={{0,8},{8,16},{16,24},{24,0},{32,40},{40,48},{48,56},{56,32},{64,72... | collective-permute-start | bytes 393224 | tf_op jit(solution)/shard_map/ppermute | solution.py:296
  30.0 25.9 %collective-permute-start.11 = (bf16[256,256]{1,0:T(8,128)(2,1)S(1)}, bf16[256,256]{1,0:T(8,128)(2,1)S(1)}, u32[]{:S(2)}, u32[]{:S(2)}) collective-permute-start(bf16[256,256]{1,0:T(8,128)(2,1)S(1)} %get-tuple-element.17), channel_id=1, source_target_pairs={{0,16},{8,24},{16,0},{24,8},{32,48},{40,56},{48,32},{56,40},{64,80... | collective-permute-start | bytes 393224 | tf_op jit(solution)/shard_map/ppermute | solution.py:296
  45.4 31.6 %collective-permute-start.22 = (bf16[512,512]{1,0:T(8,128)(2,1)S(1)}, bf16[512,512]{1,0:T(8,128)(2,1)S(1)}, u32[]{:S(2)}, u32[]{:S(2)}) collective-permute-start(bf16[512,512]{1,0:T(8,128)(2,1)S(1)} %medium.5.refs_0_), channel_id=1, source_target_pairs={{0,6},{1,7},{2,0},{3,1},{4,2},{5,3},{6,4},{7,5},{8,14},{9,15},{10,... | collective-permute-start | bytes 1572872 | tf_op jit(solution)/shard_map/ppermute | solution.py:296
  47.3 28.9 %collective-permute-start = (bf16[3,144,512]{2,1,0:T(8,128)(2,1)S(1)}, bf16[3,144,512]{2,1,0:T(8,128)(2,1)S(1)}, u32[]{:S(2)}, u32[]{:S(2)}) collective-permute-start(bf16[3,144,512]{2,1,0:T(8,128)(2,1)S(1)} %slice.43), channel_id=1, source_target_pairs={{0,8},{8,16},{16,24},{24,32},{32,40},{40,48},{48,56},{56,64},{64,7... | collective-permute-start | bytes 1327112 | tf_op jit(solution)/shard_map/ppermute | solution.py:474
  55.9 23.8 %collective-permute-start.23 = (bf16[512,512]{1,0:T(8,128)(2,1)S(1)}, bf16[512,512]{1,0:T(8,128)(2,1)S(1)}, u32[]{:S(2)}, u32[]{:S(2)}) collective-permute-start(bf16[512,512]{1,0:T(8,128)(2,1)S(1)} %medium.5.refs_0_), channel_id=1, source_target_pairs={{0,4},{1,5},{2,6},{3,7},{4,0},{5,1},{6,2},{7,3},{8,12},{9,13},{10,... | collective-permute-start | bytes 1572872 | tf_op jit(solution)/shard_map/ppermute | solution.py:296
  62.8 17.7 %collective-permute-start.24 = (bf16[512,512]{1,0:T(8,128)(2,1)S(1)}, bf16[512,512]{1,0:T(8,128)(2,1)}, u32[]{:S(2)}, u32[]{:S(2)}) collective-permute-start(bf16[512,512]{1,0:T(8,128)(2,1)S(1)} %medium.5.refs_0_), channel_id=1, source_target_pairs={{0,2},{1,3},{2,4},{3,5},{4,6},{5,7},{6,0},{7,1},{8,10},{9,11},{10,... | collective-permute-start | bytes 1572872 | tf_op jit(solution)/shard_map/ppermute | solution.py:296
  76.2 27.7 %collective-permute-start.13 = (bf16[4,256,256]{2,1,0:T(8,128)(2,1)S(1)}, bf16[4,256,256]{2,1,0:T(8,128)(2,1)S(1)}, u32[]{:S(2)}, u32[]{:S(2)}) collective-permute-start(bf16[4,256,256]{2,1,0:T(8,128)(2,1)S(1)} %pad_maximum_fusion.1.refs_8_), channel_id=1, source_target_pairs={{0,96},{8,104},{16,112},{24,120},{32,0},{40,8},{48,16},{56,24},{64... | collective-permute-start | bytes 1572872 | tf_op jit(solution)/shard_map/ppermute | solution.py:296
  77.1 36.1 %collective-permute-start.14 = (bf16[4,256,256]{2,1,0:T(8,128)(2,1)S(1)}, bf16[4,256,256]{2,1,0:T(8,128)(2,1)S(1)}, u32[]{:S(2)}, u32[]{:S(2)}) collective-permute-start(bf16[4,256,256]{2,1,0:T(8,128)(2,1)S(1)} %pad_maximum_fusion.1.refs_8_), channel_id=1, source_target_pairs={{0,64},{8,72},{16,80},{24,88},{32,96},{40,104},{48,112},{56,120},{... | collective-permute-start | bytes 1572872 | tf_op jit(solution)/shard_map/ppermute | solution.py:296
  79.7 37.2 %collective-permute-start.15 = (bf16[4,256,256]{2,1,0:T(8,128)(2,1)S(1)}, bf16[4,256,256]{2,1,0:T(8,128)(2,1)S(1)}, u32[]{:S(2)}, u32[]{:S(2)}) collective-permute-start(bf16[4,256,256]{2,1,0:T(8,128)(2,1)S(1)} %pad_maximum_fusion.1.refs_8_), channel_id=1, source_target_pairs={{0,32},{8,40},{16,48},{24,56},{32,64},{40,72},{48,80},{56,88},{64,... | collective-permute-start | bytes 1572872 | tf_op jit(solution)/shard_map/ppermute | solution.py:296
  80.5 37.2 %collective-permute-start.19 = (bf16[4,256,256]{2,1,0:T(8,128)(2,1)S(1)}, bf16[4,256,256]{2,1,0:T(8,128)(2,1)S(1)}, u32[]{:S(2)}, u32[]{:S(2)}) collective-permute-start(bf16[4,256,256]{2,1,0:T(8,128)(2,1)S(1)} %pad_maximum_fusion.2.refs_12_), channel_id=1, source_target_pairs={{0,24},{8,0},{16,8},{24,16},{32,56},{40,32},{48,40},{56,48},{64,88... | collective-permute-start | bytes 1572872 | tf_op jit(solution)/shard_map/ppermute | solution.py:296
  82.5 36.5 %collective-permute-start.20 = (bf16[4,256,256]{2,1,0:T(8,128)(2,1)S(1)}, bf16[4,256,256]{2,1,0:T(8,128)(2,1)S(1)}, u32[]{:S(2)}, u32[]{:S(2)}) collective-permute-start(bf16[4,256,256]{2,1,0:T(8,128)(2,1)S(1)} %pad_maximum_fusion.2.refs_12_), channel_id=1, source_target_pairs={{0,16},{8,24},{16,0},{24,8},{32,48},{40,56},{48,32},{56,40},{64,80... | collective-permute-start | bytes 1572872 | tf_op jit(solution)/shard_map/ppermute | solution.py:296
  113.9 25.9 %collective-permute-start.1 = (bf16[512,512]{1,0:T(8,128)(2,1)}, bf16[512,512]{1,0:T(8,128)(2,1)S(1)}, u32[]{:S(2)}, u32[]{:S(2)}) collective-permute-start(bf16[512,512]{1,0:T(8,128)(2,1)} %medium.3.refs_0_), channel_id=1, source_target_pairs={{0,6},{1,7},{2,0},{3,1},{4,2},{5,3},{6,4},{7,5},{8,14},{9,15},{10,... | collective-permute-start | bytes 1572872 | tf_op jit(solution)/shard_map/ppermute | solution.py:296
  117.7 22.1 %collective-permute-start.26 = (bf16[512,512]{1,0:T(8,128)(2,1)S(1)}, bf16[512,512]{1,0:T(8,128)(2,1)S(1)}, u32[]{:S(2)}, u32[]{:S(2)}) collective-permute-start(bf16[512,512]{1,0:T(8,128)(2,1)S(1)} %collective-permute-done.22.refs_1_), channel_id=1, source_target_pairs={{0,1},{1,0},{2,3},{3,2},{4,5},{5,4},{6,7},{7,6},{8,9},{9,8},{10,11... | collective-permute-start | bytes 1572872 | tf_op jit(solution)/shard_map/ppermute | solution.py:306
  118.5 22.1 %collective-permute-start.27 = (bf16[512,512]{1,0:T(8,128)(2,1)S(1)}, bf16[512,512]{1,0:T(8,128)(2,1)S(1)}, u32[]{:S(2)}, u32[]{:S(2)}) collective-permute-start(bf16[512,512]{1,0:T(8,128)(2,1)S(1)} %collective-permute-done.23.refs_2_), channel_id=1, source_target_pairs={{0,1},{1,0},{2,3},{3,2},{4,5},{5,4},{6,7},{7,6},{8,9},{9,8},{10,11... | collective-permute-start | bytes 1572872 | tf_op jit(solution)/shard_map/ppermute | solution.py:306
  119.8 22.2 %collective-permute-start.28 = (bf16[512,512]{1,0:T(8,128)(2,1)}, bf16[512,512]{1,0:T(8,128)(2,1)}, u32[]{:S(2)}, u32[]{:S(2)}) collective-permute-start(bf16[512,512]{1,0:T(8,128)(2,1)} %collective-permute-done.24.refs_3_), channel_id=1, source_target_pairs={{0,1},{1,0},{2,3},{3,2},{4,5},{5,4},{6,7},{7,6},{8,9},{9,8},{10,11... | collective-permute-start | bytes 1572872 | tf_op jit(solution)/shard_map/ppermute | solution.py:306
  119.8 46.5 %collective-permute-start.2 = (bf16[512,512]{1,0:T(8,128)(2,1)}, bf16[512,512]{1,0:T(8,128)(2,1)S(1)}, u32[]{:S(2)}, u32[]{:S(2)}) collective-permute-start(bf16[512,512]{1,0:T(8,128)(2,1)} %medium.3.refs_0_), channel_id=1, source_target_pairs={{0,4},{1,5},{2,6},{3,7},{4,0},{5,1},{6,2},{7,3},{8,12},{9,13},{10,... | collective-permute-start | bytes 1572872 | tf_op jit(solution)/shard_map/ppermute | solution.py:296
  139.8 26.6 %collective-permute-start.3 = (bf16[512,512]{1,0:T(8,128)(2,1)}, bf16[512,512]{1,0:T(8,128)(2,1)S(1)}, u32[]{:S(2)}, u32[]{:S(2)}) collective-permute-start(bf16[512,512]{1,0:T(8,128)(2,1)} %medium.3.refs_0_), channel_id=1, source_target_pairs={{0,2},{1,3},{2,4},{3,5},{4,6},{5,7},{6,0},{7,1},{8,10},{9,11},{10,... | collective-permute-start | bytes 1572872 | tf_op jit(solution)/shard_map/ppermute | solution.py:296
  140.6 26.3 %collective-permute-start.4 = (bf16[512,512]{1,0:T(8,128)(2,1)}, bf16[512,512]{1,0:T(8,128)(2,1)S(1)}, u32[]{:S(2)}, u32[]{:S(2)}) collective-permute-start(bf16[512,512]{1,0:T(8,128)(2,1)} %medium.3.refs_0_), channel_id=1, source_target_pairs={{0,1},{1,0},{2,3},{3,2},{4,5},{5,4},{6,7},{7,6},{8,9},{9,8},{10,11... | collective-permute-start | bytes 1572872 | tf_op jit(solution)/shard_map/ppermute | solution.py:306
  141.4 25.4 %collective-permute-start.5 = (bf16[512,512]{1,0:T(8,128)(2,1)S(1)}, bf16[512,512]{1,0:T(8,128)(2,1)S(1)}, u32[]{:S(2)}, u32[]{:S(2)}) collective-permute-start(bf16[512,512]{1,0:T(8,128)(2,1)S(1)} %collective-permute-done.1.refs_1_), channel_id=1, source_target_pairs={{0,1},{1,0},{2,3},{3,2},{4,5},{5,4},{6,7},{7,6},{8,9},{9,8},{10,11... | collective-permute-start | bytes 1572872 | tf_op jit(solution)/shard_map/ppermute | solution.py:306
  175.4 26.9 %collective-permute-start.39 = (bf16[528,512]{1,0:T(8,128)(2,1)S(1)}, bf16[528,512]{1,0:T(8,128)(2,1)}, u32[]{:S(2)}, u32[]{:S(2)}) collective-permute-start(bf16[528,512]{1,0:T(8,128)(2,1)S(1)} %get-tuple-element.12.refs_0_), channel_id=1, source_target_pairs={{0,6},{1,7},{2,0},{3,1},{4,2},{5,3},{6,4},{7,5},{8,14},{9,15},{10,... | collective-permute-start | bytes 1622024 | tf_op jit(solution)/shard_map/ppermute | solution.py:310
  178.3 17.0 %collective-permute-start.30 = (bf16[256,512]{1,0:T(8,128)(2,1)S(1)}, bf16[256,512]{1,0:T(8,128)(2,1)S(1)}, u32[]{:S(2)}, u32[]{:S(2)}) collective-permute-start(bf16[256,512]{1,0:T(8,128)(2,1)S(1)} %slice.60), channel_id=1, source_target_pairs={{0,6},{1,7},{2,0},{3,1},{4,2},{5,3},{6,4},{7,5},{8,14},{9,15},{10,... | collective-permute-start | bytes 786440 | tf_op jit(solution)/shard_map/ppermute | solution.py:312
  182.1 20.7 %collective-permute-start.41 = (bf16[528,512]{1,0:T(8,128)(2,1)S(1)}, bf16[528,512]{1,0:T(8,128)(2,1)S(1)}, u32[]{:S(2)}, u32[]{:S(2)}) collective-permute-start(bf16[528,512]{1,0:T(8,128)(2,1)S(1)} %get-tuple-element.12.refs_0_), channel_id=1, source_target_pairs={{0,2},{1,3},{2,4},{3,5},{4,6},{5,7},{6,0},{7,1},{8,10},{9,11},{10,... | collective-permute-start | bytes 1622024 | tf_op jit(solution)/shard_map/ppermute | solution.py:311
  182.4 19.9 %collective-permute-start.32 = (bf16[272,512]{1,0:T(8,128)(2,1)S(1)}, bf16[272,512]{1,0:T(8,128)(2,1)S(1)}, u32[]{:S(2)}, u32[]{:S(2)}) collective-permute-start(bf16[272,512]{1,0:T(8,128)(2,1)S(1)} %slice.61), channel_id=1, source_target_pairs={{0,2},{1,3},{2,4},{3,5},{4,6},{5,7},{6,0},{7,1},{8,10},{9,11},{10,... | collective-permute-start | bytes 835592 | tf_op jit(solution)/shard_map/ppermute | solution.py:313
  183.1 20.7 %collective-permute-start.34 = (bf16[528,512]{1,0:T(8,128)(2,1)S(1)}, bf16[528,512]{1,0:T(8,128)(2,1)S(1)}, u32[]{:S(2)}, u32[]{:S(2)}) collective-permute-start(bf16[528,512]{1,0:T(8,128)(2,1)S(1)} %collective-permute-done.29.refs_1_), channel_id=1, source_target_pairs={{0,1},{1,0},{2,3},{3,2},{4,5},{5,4},{6,7},{7,6},{8,9},{9,8},{10,11... | collective-permute-start | bytes 1622024 | tf_op jit(solution)/shard_map/ppermute | solution.py:315
  202.8 22.7 %collective-permute-start.43 = (bf16[528,512]{1,0:T(8,128)(2,1)S(1)}, bf16[528,512]{1,0:T(8,128)(2,1)}, u32[]{:S(2)}, u32[]{:S(2)}) collective-permute-start(bf16[528,512]{1,0:T(8,128)(2,1)S(1)} %get-tuple-element.12.refs_0_), channel_id=1, source_target_pairs={{0,1},{1,0},{2,3},{3,2},{4,5},{5,4},{6,7},{7,6},{8,9},{9,8},{10,11... | collective-permute-start | bytes 1622024 | tf_op jit(solution)/shard_map/ppermute | solution.py:315
  203.8 24.9 %collective-permute-start.44 = (bf16[528,512]{1,0:T(8,128)(2,1)}, bf16[528,512]{1,0:T(8,128)(2,1)}, u32[]{:S(2)}, u32[]{:S(2)}) collective-permute-start(bf16[528,512]{1,0:T(8,128)(2,1)} %collective-permute-done.39.refs_1_), channel_id=1, source_target_pairs={{0,1},{1,0},{2,3},{3,2},{4,5},{5,4},{6,7},{7,6},{8,9},{9,8},{10,11... | collective-permute-start | bytes 1622024 | tf_op jit(solution)/shard_map/ppermute | solution.py:315
  204.0 24.7 %collective-permute-start.47 = (bf16[528,512]{1,0:T(8,128)(2,1)S(1)}, bf16[528,512]{1,0:T(8,128)(2,1)}, u32[]{:S(2)}, u32[]{:S(2)}) collective-permute-start(bf16[528,512]{1,0:T(8,128)(2,1)S(1)} %collective-permute-done.41.refs_4_), channel_id=1, source_target_pairs={{0,1},{1,0},{2,3},{3,2},{4,5},{5,4},{6,7},{7,6},{8,9},{9,8},{10,11... | collective-permute-start | bytes 1622024 | tf_op jit(solution)/shard_map/ppermute | solution.py:315
  253.1 26.7 %collective-permute-start.54 = (bf16[16,512]{1,0:T(8,128)(2,1)S(1)}, bf16[16,512]{1,0:T(8,128)(2,1)S(1)}, u32[]{:S(2)}, u32[]{:S(2)}) collective-permute-start(bf16[16,512]{1,0:T(8,128)(2,1)S(1)} %fusion.15), channel_id=1, source_target_pairs={{0,32},{8,40},{16,48},{24,56},{32,64},{40,72},{48,80},{56,88},{64,... | collective-permute-start | bytes 49160 | tf_op jit(solution)/shard_map/ppermute | solution.py:296
  259.7 20.0 %collective-permute-start.53 = (bf16[16,512]{1,0:T(8,128)(2,1)S(1)}, bf16[16,512]{1,0:T(8,128)(2,1)S(1)}, u32[]{:S(2)}, u32[]{:S(2)}) collective-permute-start(bf16[16,512]{1,0:T(8,128)(2,1)S(1)} %fusion.15), channel_id=1, source_target_pairs={{0,64},{8,72},{16,80},{24,88},{32,96},{40,104},{48,112},{56,120},{... | collective-permute-start | bytes 49160 | tf_op jit(solution)/shard_map/ppermute | solution.py:296
  259.8 20.0 %collective-permute-start.52 = (bf16[16,512]{1,0:T(8,128)(2,1)S(1)}, bf16[16,512]{1,0:T(8,128)(2,1)S(1)}, u32[]{:S(2)}, u32[]{:S(2)}) collective-permute-start(bf16[16,512]{1,0:T(8,128)(2,1)S(1)} %fusion.15), channel_id=1, source_target_pairs={{0,96},{8,104},{16,112},{24,120},{32,0},{40,8},{48,16},{56,24},{64... | collective-permute-start | bytes 49160 | tf_op jit(solution)/shard_map/ppermute | solution.py:296
  (88 other events, 1008.6 us)
Sparse Core Ops, SparseCore 0:
  10.1 98.7 all-gather.6
  111.0 61.1 all-gather.4

commit v2 on v1

--- a/solution.py
+++ b/solution.py
@@ -474,8 +474,9 @@
     rim = lax.ppermute(qkv_first[:, length - HALO :], "ctx", ahead)
     first = jnp.where(odd == 0, turned[0], turned[1])
     second = jnp.where(odd == 0, turned[1], turned[0])
-    weight = lax.all_gather(in_weight[1:], "ctx")
-    query_weight = lax.all_gather(in_weight[:1], "ctx")
+    late_weight, first, second = lax.optimization_barrier((in_weight, first, second))
+    weight = lax.all_gather(late_weight[1:], "ctx")
+    query_weight = lax.all_gather(late_weight[:1], "ctx")
     out_west = plane_gather(first, x_pairs, y_pairs)
     out_south = plane_gather(second, y_pairs, x_pairs)
 

time: 301 us -> 311 us (1.033)
  waiting for transfers between devices: 77.1 us -> 87.5 us
    ppermute x24, waiting for transfers between devices: 44.2 us -> 53.2 us  [ring(): return [a] + [lax.ppermute(a, axis, pairs(-d)) for d in (1, 2, 3)]]
    unnamed x130 -> x132, local copies, waits for them, and re-layouts: 25.5 us -> 25.5 us
  transfers between devices with their start and end apart: 57 -> 57, of which waited for: 18 -> 20; matrix products, arithmetic and copies ran while one was open for 4% -> 3% of each run, Pallas kernels for 25% -> 24%
where the time goes in v2:
time: 311 us; the launch traced here: 305 us
  waiting for transfers between devices  87.5 us (28%)
  starting transfers between devices  81.9 us (26%)
  Pallas kernels  81.8 us (26%)
  local copies, waits for them, and re-layouts  34.8 us (11%)
  between operations  14.9 us (5%)
  other arithmetic  4.29 us (1%)
    ppermute x24, waiting for transfers between devices, ring(): return [a] + [lax.ppermute(a, axis, pairs(-d)) for d in (1, 2, 3)]  53.2 us
    ppermute x24, starting transfers between devices, ring(): return [a] + [lax.ppermute(a, axis, pairs(-d)) for d in (1, 2, 3)]  46.4 us
    pallas_call x4, Pallas kernels, project(): pl.pallas_call(project_kernel, out_shape=jax.ShapeDtypeStruct((count, row...  34 us
    unnamed x132, local copies, waits for them, and re-layouts  25.5 us
    pallas_call x3, Pallas kernels, medium(): pl.pallas_call(conv_kernel, out_shape=jax.ShapeDtypeStruct((length, chann...  23.2 us
    ppermute x2, waiting for transfers between devices, token_gather(): low = lax.ppermute(after[:HALF], 'tp', z_pairs(-1))  12.6 us
    ppermute x2, waiting for transfers between devices, token_gather(): high = lax.ppermute(before[HALF:], 'tp', z_pairs(1))  11.9 us
    pallas_call x2, Pallas kernels, mix(): pl.pallas_call(mix_kernel, out_shape=(jax.ShapeDtypeStruct((rows, channel...  10.9 us
  transfers between devices with their start and end apart: 57, of which 20 were waited for; matrix products, arithmetic and copies ran while one was open for 3% of the time, Pallas kernels for 24%

profile of v2, /device:TPU:28, one launch (start us, length us, event | category | flops | bytes accessed | tf_op | source)
XLA Modules:
  0.0 305.1 jit_solution(5333608812973149564)
XLA Ops:
  8.2 3.2 %collective-permute-start.9 = (bf16[256,256]{1,0:T(8,128)(2,1)S(1)}, bf16[256,256]{1,0:T(8,128)(2,1)S(1)}, u32[]{:S(2)}, u32[]{:S(2)}) collective-permute-start(bf16[256,256]{1,0:T(8,128)(2,1)S(1)} %get-tuple-element.24), channel_id=1, source_target_pairs={{0,8},{1,24},{2,40},{3,56},{4,72},{5,88},{6,104},{7,120},{8,0},{9,... | collective-permute-start | bytes 393224 | tf_op jit(solution)/shard_map/ppermute | solution.py:473
  11.4 6.0 %collective-permute-start.8 = (bf16[256,256]{1,0:T(8,128)(2,1)S(1)}, bf16[256,256]{1,0:T(8,128)(2,1)S(1)}, u32[]{:S(2)}, u32[]{:S(2)}) collective-permute-start(bf16[256,256]{1,0:T(8,128)(2,1)S(1)} %get-tuple-element.25), channel_id=1, source_target_pairs={{0,0},{1,16},{2,32},{3,48},{4,64},{5,80},{6,96},{7,112},{8,8},{9,2... | collective-permute-start | bytes 393224 | tf_op jit(solution)/shard_map/ppermute | solution.py:473
  18.5 5.9 %collective-permute-done.8 = bf16[256,256]{1,0:T(8,128)(2,1)S(1)} collective-permute-done((bf16[256,256]{1,0:T(8,128)(2,1)S(1)}, bf16[256,256]{1,0:T(8,128)(2,1)S(1)}, u32[]{:S(2)}, u32[]{:S(2)}) %collective-permute-start.8) | collective-permute-done | bytes 131104 | tf_op jit(solution)/shard_map/ppermute | solution.py:473
  35.2 5.7 %medium.4.refs_0_ = bf16[512,512]{1,0:T(8,128)(2,1)S(1)} custom-call(bf16[3,1024,512]{2,1,0:T(8,128)(2,1)S(1)} %copy-done, bf16[3,1024,512]{2,1,0:T(8,128)(2,1)S(1)} %copy-done, f32[3,3,512]{2,1,0:T(4,128)S(1)} %copy-done.46, f32[9,32,512]{2,1,0:T(8,128)S(1)} %add_dynamic-update-slice_fusion.filt_ref), custom_call_target="tpu_custom_call" | custom-call | tf_op jit(solution)/shard_map/medium/pallas_call | solution.py:91
  40.9 5.7 %medium.5.refs_0_ = bf16[512,512]{1,0:T(8,128)(2,1)S(1)} custom-call(bf16[3,1024,512]{2,1,0:T(8,128)(2,1)S(1)} %copy-done, bf16[3,1024,512]{2,1,0:T(8,128)(2,1)S(1)} %copy-done, f32[3,3,512]{2,1,0:T(4,128)S(1)} %copy-done.46, f32[9,32,512]{2,1,0:T(8,128)S(1)} %add_dynamic-update-slice_fusion.filt_ref, ...), custom_call_target="tpu_custom_call", output_to_operand_aliasing={{}: (4, {})} | custom-call | tf_op jit(solution)/shard_map/medium/pallas_call | solution.py:91
  47.8 2.9 collective-permute-start
  50.7 5.6 %collective-permute-start.18 = (bf16[256,256]{1,0:T(8,128)(2,1)S(1)}, bf16[256,256]{1,0:T(8,128)(2,1)S(1)}, u32[]{:S(2)}, u32[]{:S(2)}) collective-permute-start(bf16[256,256]{1,0:T(8,128)(2,1)S(1)} %copy-done.61), channel_id=1, source_target_pairs={{0,32},{8,40},{16,48},{24,56},{32,64},{40,72},{48,80},{56,88},{64,... | collective-permute-start | bytes 393224 | tf_op jit(solution)/shard_map/ppermute | solution.py:296
  56.6 4.0 %collective-permute-done.18 = bf16[256,256]{1,0:T(8,128)(2,1)S(1)} collective-permute-done((bf16[256,256]{1,0:T(8,128)(2,1)S(1)}, bf16[256,256]{1,0:T(8,128)(2,1)S(1)}, u32[]{:S(2)}, u32[]{:S(2)}) %collective-permute-start.18) | collective-permute-done | bytes 131104 | tf_op jit(solution)/shard_map/ppermute | solution.py:296
  63.0 6.1 %collective-permute-done.16 = bf16[256,256]{1,0:T(8,128)(2,1)S(1)} collective-permute-done((bf16[256,256]{1,0:T(8,128)(2,1)S(1)}, bf16[256,256]{1,0:T(8,128)(2,1)S(1)}, u32[]{:S(2)}, u32[]{:S(2)}) %collective-permute-start.16) | collective-permute-done | bytes 131104 | tf_op jit(solution)/shard_map/ppermute | solution.py:296
  73.2 7.7 %collective-permute-done.24.refs_3_ = bf16[512,512]{1,0:T(8,128)(2,1)} collective-permute-done((bf16[512,512]{1,0:T(8,128)(2,1)S(1)}, bf16[512,512]{1,0:T(8,128)(2,1)}, u32[]{:S(2)}, u32[]{:S(2)}) %collective-permute-start.24) | collective-permute-done | bytes 524320 | tf_op jit(solution)/shard_map/ppermute | solution.py:296
  83.0 6.1 %collective-permute-start.20 = (bf16[4,256,256]{2,1,0:T(8,128)(2,1)S(1)}, bf16[4,256,256]{2,1,0:T(8,128)(2,1)S(1)}, u32[]{:S(2)}, u32[]{:S(2)}) collective-permute-start(bf16[4,256,256]{2,1,0:T(8,128)(2,1)S(1)} %pad_maximum_fusion.2.refs_12_), channel_id=1, source_target_pairs={{0,16},{8,24},{16,0},{24,8},{32,48},{40,56},{48,32},{56,40},{64,80... | collective-permute-start | bytes 1572872 | tf_op jit(solution)/shard_map/ppermute | solution.py:296
  89.1 11.9 %medium.3.refs_0_ = bf16[512,512]{1,0:T(8,128)(2,1)} custom-call(bf16[3,144,512]{2,1,0:T(8,128)(2,1)S(1)} %collective-permute-done.prev_ref, bf16[3,1024,512]{2,1,0:T(8,128)(2,1)S(1)} %copy-done, f32[3,3,512]{2,1,0:T(4,128)S(1)} %copy-done.46, f32[9,32,512]{2,1,0:T(8,128)S(1)} %add_dynamic-update-slice_fusion.filt_ref), custom_call_target="tpu_custom_call" | custom-call | tf_op jit(solution)/shard_map/medium/pallas_call | solution.py:91
  104.3 12.8 %collective-permute-done.14.refs_10_ = bf16[4,256,256]{2,1,0:T(8,128)(2,1)S(1)} collective-permute-done((bf16[4,256,256]{2,1,0:T(8,128)(2,1)S(1)}, bf16[4,256,256]{2,1,0:T(8,128)(2,1)S(1)}, u32[]{:S(2)}, u32[]{:S(2)}) %collective-permute-start.14) | collective-permute-done | bytes 524320 | tf_op jit(solution)/shard_map/ppermute | solution.py:296
  117.9 3.3 %collective-permute-start.1 = (bf16[512,512]{1,0:T(8,128)(2,1)}, bf16[512,512]{1,0:T(8,128)(2,1)S(1)}, u32[]{:S(2)}, u32[]{:S(2)}) collective-permute-start(bf16[512,512]{1,0:T(8,128)(2,1)} %medium.3.refs_0_), channel_id=1, source_target_pairs={{0,6},{1,7},{2,0},{3,1},{4,2},{5,3},{6,4},{7,5},{8,14},{9,15},{10,... | collective-permute-start | bytes 1572872 | tf_op jit(solution)/shard_map/ppermute | solution.py:296
  124.1 3.3 %collective-permute-done.21.refs_15_ = bf16[4,256,256]{2,1,0:T(8,128)(2,1)S(1)} collective-permute-done((bf16[4,256,256]{2,1,0:T(8,128)(2,1)S(1)}, bf16[4,256,256]{2,1,0:T(8,128)(2,1)S(1)}, u32[]{:S(2)}, u32[]{:S(2)}) %collective-permute-start.21) | collective-permute-done | bytes 524320 | tf_op jit(solution)/shard_map/ppermute | solution.py:296
  129.5 14.2 %collective-permute-done.1.refs_1_ = bf16[512,512]{1,0:T(8,128)(2,1)S(1)} collective-permute-done((bf16[512,512]{1,0:T(8,128)(2,1)}, bf16[512,512]{1,0:T(8,128)(2,1)S(1)}, u32[]{:S(2)}, u32[]{:S(2)}) %collective-permute-start.1) | collective-permute-done | bytes 524320 | tf_op jit(solution)/shard_map/ppermute | solution.py:296
  160.8 5.6 %mix.3 = (bf16[512,512]{1,0:T(8,128)(2,1)S(1)}, bf16[528,512]{1,0:T(8,128)(2,1)S(1)}) custom-call(s32[4]{0:T(128)S(1)} %pad_add_fusion.place_ref, bf16[512,512]{1,0:T(8,128)(2,1)S(1)} %copy-done.2, bf16[512,512]{1,0:T(8,128)(2,1)S(1)} %copy-done.35, bf16[512,512]{1,0:T(8,128)(2,1)S(1)} %copy-done.37, bf16[512,512]{1,0:T(8,128)(2,1)} %collective-permute-done.24.refs_3_, ...), custom_call_target="tpu_custom_call" | custom-call | tf_op jit(solution)/shard_map/mix/pallas_call | solution.py:368
  166.5 3.6 %collective-permute-start.29 = (bf16[528,512]{1,0:T(8,128)(2,1)S(1)}, bf16[528,512]{1,0:T(8,128)(2,1)S(1)}, u32[]{:S(2)}, u32[]{:S(2)}) collective-permute-start(bf16[528,512]{1,0:T(8,128)(2,1)S(1)} %get-tuple-element.16.refs_0_), channel_id=1, source_target_pairs={{0,6},{1,7},{2,0},{3,1},{4,2},{5,3},{6,4},{7,5},{8,14},{9,15},{10,... | collective-permute-start | bytes 1622024 | tf_op jit(solution)/shard_map/ppermute | solution.py:310
  173.9 5.2 %mix.2 = (bf16[512,512]{1,0:T(8,128)(2,1)S(1)}, bf16[528,512]{1,0:T(8,128)(2,1)S(1)}) custom-call(s32[4]{0:T(128)S(1)} %pad_add_fusion.place_ref, bf16[512,512]{1,0:T(8,128)(2,1)} %medium.3.refs_0_, bf16[512,512]{1,0:T(8,128)(2,1)S(1)} %collective-permute-done.1.refs_1_, bf16[512,512]{1,0:T(8,128)(2,1)S(1)} %collective-permute-done.2.refs_2_, ...), custom_call_target="tpu_custom_call" | custom-call | tf_op jit(solution)/shard_map/mix/pallas_call | solution.py:368
  181.9 3.8 %collective-permute-start.30 = (bf16[256,512]{1,0:T(8,128)(2,1)S(1)}, bf16[256,512]{1,0:T(8,128)(2,1)S(1)}, u32[]{:S(2)}, u32[]{:S(2)}) collective-permute-start(bf16[256,512]{1,0:T(8,128)(2,1)S(1)} %slice.60), channel_id=1, source_target_pairs={{0,6},{1,7},{2,0},{3,1},{4,2},{5,3},{6,4},{7,5},{8,14},{9,15},{10,... | collective-permute-start | bytes 786440 | tf_op jit(solution)/shard_map/ppermute | solution.py:312
  187.3 11.8 %collective-permute-done.30.refs_2_ = bf16[256,512]{1,0:T(8,128)(2,1)S(1)} collective-permute-done((bf16[256,512]{1,0:T(8,128)(2,1)S(1)}, bf16[256,512]{1,0:T(8,128)(2,1)S(1)}, u32[]{:S(2)}, u32[]{:S(2)}) %collective-permute-start.30) | collective-permute-done | bytes 262176 | tf_op jit(solution)/shard_map/ppermute | solution.py:312
  199.1 6.8 %collective-permute-done.32.refs_3_ = bf16[272,512]{1,0:T(8,128)(2,1)S(1)} collective-permute-done((bf16[272,512]{1,0:T(8,128)(2,1)S(1)}, bf16[272,512]{1,0:T(8,128)(2,1)S(1)}, u32[]{:S(2)}, u32[]{:S(2)}) %collective-permute-start.32) | collective-permute-done | bytes 278560 | tf_op jit(solution)/shard_map/ppermute | solution.py:313
  209.2 3.2 %collective-permute-start.40 = (bf16[256,512]{1,0:T(8,128)(2,1)S(1)}, bf16[256,512]{1,0:T(8,128)(2,1)}, u32[]{:S(2)}, u32[]{:S(2)}) collective-permute-start(bf16[256,512]{1,0:T(8,128)(2,1)S(1)} %slice.63), channel_id=1, source_target_pairs={{0,6},{1,7},{2,0},{3,1},{4,2},{5,3},{6,4},{7,5},{8,14},{9,15},{10,... | collective-permute-start | bytes 786440 | tf_op jit(solution)/shard_map/ppermute | solution.py:312
  212.4 5.1 %collective-permute-done.42.refs_3_ = bf16[272,512]{1,0:T(8,128)(2,1)} collective-permute-done((bf16[272,512]{1,0:T(8,128)(2,1)S(1)}, bf16[272,512]{1,0:T(8,128)(2,1)}, u32[]{:S(2)}, u32[]{:S(2)}) %collective-permute-start.42) | collective-permute-done | bytes 278560 | tf_op jit(solution)/shard_map/ppermute | solution.py:313
  218.3 10.1 %project.6.upper_ref = bf16[2,512,512]{2,1,0:T(8,128)(2,1)} custom-call(s32[4]{0:T(128)} %copy-done.49, bf16[528,512]{1,0:T(8,128)(2,1)} %copy-done.13, bf16[528,512]{1,0:T(8,128)(2,1)} %copy-done.53, bf16[256,512]{1,0:T(8,128)(2,1)} %copy-done.59, bf16[272,512]{1,0:T(8,128)(2,1)} %copy-done.57, bf16[528,512]{1,0:T(8,128)(2,1)} %copy-done.51, ...), custom_call_target="tpu_custom_call" | custom-call | tf_op jit(solution)/shard_map/project/pallas_call | solution.py:428
  229.1 3.9 %collective-permute-start.48 = (bf16[2,16,512]{2,1,0:T(8,128)(2,1)S(1)}, bf16[2,16,512]{2,1,0:T(8,128)(2,1)S(1)}, u32[]{:S(2)}, u32[]{:S(2)}) collective-permute-start(bf16[2,16,512]{2,1,0:T(8,128)(2,1)S(1)} %slice.65), channel_id=1, source_target_pairs={{0,8},{8,16},{16,24},{24,32},{32,40},{40,48},{48,56},{56,64},{64,7... | collective-permute-start | bytes 98312 | tf_op jit(solution)/shard_map/ppermute | solution.py:499
  233.1 10.1 %project.7.lower_ref = bf16[2,512,512]{2,1,0:T(8,128)(2,1)} custom-call(s32[4]{0:T(128)} %copy-done.49, bf16[528,512]{1,0:T(8,128)(2,1)} %copy-done.14, bf16[528,512]{1,0:T(8,128)(2,1)} %collective-permute-done.39.refs_1_, bf16[256,512]{1,0:T(8,128)(2,1)} %collective-permute-done.40.refs_2_, bf16[272,512]{1,0:T(8,128)(2,1)} %collective-permute-done.42.refs_3_, ...), custom_call_target="tpu_custom_call" | custom-call | tf_op jit(solution)/shard_map/project/pallas_call | solution.py:428
  244.4 6.3 %modal_scan.1 = (f32[128,8,512]{2,1,0:T(8,128)S(1)}, f32[16,8,512]{2,1,0:T(8,128)S(1)}, bf16[16,512]{1,0:T(8,128)(2,1)S(1)}) custom-call(bf16[2,16,512]{2,1,0:T(8,128)(2,1)S(1)} %collective-permute-done.48.edge_ref, bf16[2,512,512]{2,1,0:T(8,128)(2,1)S(1)} %copy-done.10, bf16[2,512,512]{2,1,0:T(8,128)(2,1)S(1)} %copy-done.9, f32[3,3,512]{2,1,0:T(4,128)S(1)} %copy-done.47, ...), custom_call_target="tpu_custom_call" | custom-call | tf_op jit(solution)/shard_map/modal_scan/pallas_call | solution.py:181
  256.4 13.2 %collective-permute-start.54 = (bf16[16,512]{1,0:T(8,128)(2,1)S(1)}, bf16[16,512]{1,0:T(8,128)(2,1)S(1)}, u32[]{:S(2)}, u32[]{:S(2)}) collective-permute-start(bf16[16,512]{1,0:T(8,128)(2,1)S(1)} %fusion.15), channel_id=1, source_target_pairs={{0,32},{8,40},{16,48},{24,56},{32,64},{40,72},{48,80},{56,88},{64,... | collective-permute-start | bytes 49160 | tf_op jit(solution)/shard_map/ppermute | solution.py:296
  272.8 6.9 %project.4.upper_ref = bf16[1,512,512]{2,1,0:T(8,128)(2,1)} custom-call(s32[4]{0:T(128)} %copy-done.49, bf16[528,512]{1,0:T(8,128)(2,1)} %copy-done.13, bf16[528,512]{1,0:T(8,128)(2,1)} %copy-done.53, bf16[256,512]{1,0:T(8,128)(2,1)} %copy-done.59, bf16[272,512]{1,0:T(8,128)(2,1)} %copy-done.57, bf16[528,512]{1,0:T(8,128)(2,1)} %copy-done.51, ...), custom_call_target="tpu_custom_call" | custom-call | tf_op jit(solution)/shard_map/project/pallas_call | solution.py:428
  282.7 6.9 %project.5.lower_ref = bf16[1,512,512]{2,1,0:T(8,128)(2,1)} custom-call(s32[4]{0:T(128)} %copy-done.49, bf16[528,512]{1,0:T(8,128)(2,1)} %copy-done.14, bf16[528,512]{1,0:T(8,128)(2,1)} %collective-permute-done.39.refs_1_, bf16[256,512]{1,0:T(8,128)(2,1)} %collective-permute-done.40.refs_2_, bf16[272,512]{1,0:T(8,128)(2,1)} %collective-permute-done.42.refs_3_, ...), custom_call_target="tpu_custom_call" | custom-call | tf_op jit(solution)/shard_map/project/pallas_call | solution.py:428
  290.8 7.5 %modal_finish.1 = bf16[1024,512]{1,0:T(8,128)(2,1)} custom-call(bf16[1,16,512]{2,1,0:T(8,128)(2,1)S(1)} %collective-permute-done.38.edge_ref, bf16[1,512,512]{2,1,0:T(8,128)(2,1)S(1)} %copy-done.15, bf16[1,512,512]{2,1,0:T(8,128)(2,1)S(1)} %copy-done.12, f32[3,3,512]{2,1,0:T(4,128)S(1)} %copy-done.47, f32[16,512]{1,0:T(8,128)S(1)} %copy-done.31, ...), custom_call_target="tpu_custom_call" | custom-call | tf_op jit(solution)/shard_map/modal_finish/pallas_call | solution.py:246
  (254 shorter events, 75.8 us)
Async XLA Ops:
  7.2 211.1 %all-gather.7.cloned.1.call-start = ((), (), s32[]{:S(2)}) async-start(), calls=%async_computation.1 | async-start | bytes 8912896 | tf_op jit(solution)/shard_map/all_gather | solution.py:478
  27.1 245.8 %all-gather.5.cloned.1.call-start = ((), (), s32[]{:S(2)}) async-start(), calls=%async_computation | async-start | bytes 4456448 | tf_op jit(solution)/shard_map/all_gather | solution.py:479
  32.1 18.6 %collective-permute-start.12 = (bf16[256,256]{1,0:T(8,128)(2,1)}, bf16[256,256]{1,0:T(8,128)(2,1)S(1)}, u32[]{:S(2)}, u32[]{:S(2)}) collective-permute-start(bf16[256,256]{1,0:T(8,128)(2,1)} %get-tuple-element.12), channel_id=1, source_target_pairs={{0,8},{8,16},{16,24},{24,0},{32,40},{40,48},{48,56},{56,32},{64,72... | collective-permute-start | bytes 393224 | tf_op jit(solution)/shard_map/ppermute | solution.py:296
  33.0 23.3 %collective-permute-start.11 = (bf16[256,256]{1,0:T(8,128)(2,1)}, bf16[256,256]{1,0:T(8,128)(2,1)S(1)}, u32[]{:S(2)}, u32[]{:S(2)}) collective-permute-start(bf16[256,256]{1,0:T(8,128)(2,1)} %get-tuple-element.12), channel_id=1, source_target_pairs={{0,16},{8,24},{16,0},{24,8},{32,48},{40,56},{48,32},{56,40},{64,80... | collective-permute-start | bytes 393224 | tf_op jit(solution)/shard_map/ppermute | solution.py:296
  46.6 22.7 %collective-permute-start.22 = (bf16[512,512]{1,0:T(8,128)(2,1)S(1)}, bf16[512,512]{1,0:T(8,128)(2,1)S(1)}, u32[]{:S(2)}, u32[]{:S(2)}) collective-permute-start(bf16[512,512]{1,0:T(8,128)(2,1)S(1)} %medium.5.refs_0_), channel_id=1, source_target_pairs={{0,6},{1,7},{2,0},{3,1},{4,2},{5,3},{6,4},{7,5},{8,14},{9,15},{10,... | collective-permute-start | bytes 1572872 | tf_op jit(solution)/shard_map/ppermute | solution.py:296
  47.8 21.4 %collective-permute-start = (bf16[3,144,512]{2,1,0:T(8,128)(2,1)S(1)}, bf16[3,144,512]{2,1,0:T(8,128)(2,1)S(1)}, u32[]{:S(2)}, u32[]{:S(2)}) collective-permute-start(bf16[3,144,512]{2,1,0:T(8,128)(2,1)S(1)} %slice.43), channel_id=1, source_target_pairs={{0,8},{8,16},{16,24},{24,32},{32,40},{40,48},{48,56},{56,64},{64,7... | collective-permute-start | bytes 1327112 | tf_op jit(solution)/shard_map/ppermute | solution.py:474
  60.6 20.3 %collective-permute-start.24 = (bf16[512,512]{1,0:T(8,128)(2,1)S(1)}, bf16[512,512]{1,0:T(8,128)(2,1)}, u32[]{:S(2)}, u32[]{:S(2)}) collective-permute-start(bf16[512,512]{1,0:T(8,128)(2,1)S(1)} %medium.5.refs_0_), channel_id=1, source_target_pairs={{0,2},{1,3},{2,4},{3,5},{4,6},{5,7},{6,0},{7,1},{8,10},{9,11},{10,... | collective-permute-start | bytes 1572872 | tf_op jit(solution)/shard_map/ppermute | solution.py:296
  69.2 31.8 %collective-permute-start.13 = (bf16[4,256,256]{2,1,0:T(8,128)(2,1)S(1)}, bf16[4,256,256]{2,1,0:T(8,128)(2,1)S(1)}, u32[]{:S(2)}, u32[]{:S(2)}) collective-permute-start(bf16[4,256,256]{2,1,0:T(8,128)(2,1)S(1)} %pad_maximum_fusion.1.refs_8_), channel_id=1, source_target_pairs={{0,96},{8,104},{16,112},{24,120},{32,0},{40,8},{48,16},{56,24},{64... | collective-permute-start | bytes 1572872 | tf_op jit(solution)/shard_map/ppermute | solution.py:296
  69.3 47.8 %collective-permute-start.14 = (bf16[4,256,256]{2,1,0:T(8,128)(2,1)S(1)}, bf16[4,256,256]{2,1,0:T(8,128)(2,1)S(1)}, u32[]{:S(2)}, u32[]{:S(2)}) collective-permute-start(bf16[4,256,256]{2,1,0:T(8,128)(2,1)S(1)} %pad_maximum_fusion.1.refs_8_), channel_id=1, source_target_pairs={{0,64},{8,72},{16,80},{24,88},{32,96},{40,104},{48,112},{56,120},{... | collective-permute-start | bytes 1572872 | tf_op jit(solution)/shard_map/ppermute | solution.py:296
  72.7 48.5 %collective-permute-start.15 = (bf16[4,256,256]{2,1,0:T(8,128)(2,1)S(1)}, bf16[4,256,256]{2,1,0:T(8,128)(2,1)S(1)}, u32[]{:S(2)}, u32[]{:S(2)}) collective-permute-start(bf16[4,256,256]{2,1,0:T(8,128)(2,1)S(1)} %pad_maximum_fusion.1.refs_8_), channel_id=1, source_target_pairs={{0,32},{8,40},{16,48},{24,56},{32,64},{40,72},{48,80},{56,88},{64,... | collective-permute-start | bytes 1572872 | tf_op jit(solution)/shard_map/ppermute | solution.py:296
  81.0 41.1 %collective-permute-start.19 = (bf16[4,256,256]{2,1,0:T(8,128)(2,1)S(1)}, bf16[4,256,256]{2,1,0:T(8,128)(2,1)S(1)}, u32[]{:S(2)}, u32[]{:S(2)}) collective-permute-start(bf16[4,256,256]{2,1,0:T(8,128)(2,1)S(1)} %pad_maximum_fusion.2.refs_12_), channel_id=1, source_target_pairs={{0,24},{8,0},{16,8},{24,16},{32,56},{40,32},{48,40},{56,48},{64,88... | collective-permute-start | bytes 1572872 | tf_op jit(solution)/shard_map/ppermute | solution.py:296
  83.0 40.4 %collective-permute-start.20 = (bf16[4,256,256]{2,1,0:T(8,128)(2,1)S(1)}, bf16[4,256,256]{2,1,0:T(8,128)(2,1)S(1)}, u32[]{:S(2)}, u32[]{:S(2)}) collective-permute-start(bf16[4,256,256]{2,1,0:T(8,128)(2,1)S(1)} %pad_maximum_fusion.2.refs_12_), channel_id=1, source_target_pairs={{0,16},{8,24},{16,0},{24,8},{32,48},{40,56},{48,32},{56,40},{64,80... | collective-permute-start | bytes 1572872 | tf_op jit(solution)/shard_map/ppermute | solution.py:296
  101.8 25.7 %collective-permute-start.21 = (bf16[4,256,256]{2,1,0:T(8,128)(2,1)S(1)}, bf16[4,256,256]{2,1,0:T(8,128)(2,1)S(1)}, u32[]{:S(2)}, u32[]{:S(2)}) collective-permute-start(bf16[4,256,256]{2,1,0:T(8,128)(2,1)S(1)} %pad_maximum_fusion.2.refs_12_), channel_id=1, source_target_pairs={{0,8},{8,16},{16,24},{24,0},{32,40},{40,48},{48,56},{56,32},{64,72... | collective-permute-start | bytes 1572872 | tf_op jit(solution)/shard_map/ppermute | solution.py:296
  117.9 25.8 %collective-permute-start.1 = (bf16[512,512]{1,0:T(8,128)(2,1)}, bf16[512,512]{1,0:T(8,128)(2,1)S(1)}, u32[]{:S(2)}, u32[]{:S(2)}) collective-permute-start(bf16[512,512]{1,0:T(8,128)(2,1)} %medium.3.refs_0_), channel_id=1, source_target_pairs={{0,6},{1,7},{2,0},{3,1},{4,2},{5,3},{6,4},{7,5},{8,14},{9,15},{10,... | collective-permute-start | bytes 1572872 | tf_op jit(solution)/shard_map/ppermute | solution.py:296
  122.0 21.7 %collective-permute-start.26 = (bf16[512,512]{1,0:T(8,128)(2,1)S(1)}, bf16[512,512]{1,0:T(8,128)(2,1)S(1)}, u32[]{:S(2)}, u32[]{:S(2)}) collective-permute-start(bf16[512,512]{1,0:T(8,128)(2,1)S(1)} %collective-permute-done.22.refs_1_), channel_id=1, source_target_pairs={{0,1},{1,0},{2,3},{3,2},{4,5},{5,4},{6,7},{7,6},{8,9},{9,8},{10,11... | collective-permute-start | bytes 1572872 | tf_op jit(solution)/shard_map/ppermute | solution.py:306
  122.8 21.7 %collective-permute-start.27 = (bf16[512,512]{1,0:T(8,128)(2,1)S(1)}, bf16[512,512]{1,0:T(8,128)(2,1)S(1)}, u32[]{:S(2)}, u32[]{:S(2)}) collective-permute-start(bf16[512,512]{1,0:T(8,128)(2,1)S(1)} %collective-permute-done.23.refs_2_), channel_id=1, source_target_pairs={{0,1},{1,0},{2,3},{3,2},{4,5},{5,4},{6,7},{7,6},{8,9},{9,8},{10,11... | collective-permute-start | bytes 1572872 | tf_op jit(solution)/shard_map/ppermute | solution.py:306
  124.1 21.8 %collective-permute-start.28 = (bf16[512,512]{1,0:T(8,128)(2,1)}, bf16[512,512]{1,0:T(8,128)(2,1)}, u32[]{:S(2)}, u32[]{:S(2)}) collective-permute-start(bf16[512,512]{1,0:T(8,128)(2,1)} %collective-permute-done.24.refs_3_), channel_id=1, source_target_pairs={{0,1},{1,0},{2,3},{3,2},{4,5},{5,4},{6,7},{7,6},{8,9},{9,8},{10,11... | collective-permute-start | bytes 1572872 | tf_op jit(solution)/shard_map/ppermute | solution.py:306
  127.4 42.7 %collective-permute-start.2 = (bf16[512,512]{1,0:T(8,128)(2,1)}, bf16[512,512]{1,0:T(8,128)(2,1)S(1)}, u32[]{:S(2)}, u32[]{:S(2)}) collective-permute-start(bf16[512,512]{1,0:T(8,128)(2,1)} %medium.3.refs_0_), channel_id=1, source_target_pairs={{0,4},{1,5},{2,6},{3,7},{4,0},{5,1},{6,2},{7,3},{8,12},{9,13},{10,... | collective-permute-start | bytes 1572872 | tf_op jit(solution)/shard_map/ppermute | solution.py:296
  143.7 26.4 %collective-permute-start.3 = (bf16[512,512]{1,0:T(8,128)(2,1)}, bf16[512,512]{1,0:T(8,128)(2,1)S(1)}, u32[]{:S(2)}, u32[]{:S(2)}) collective-permute-start(bf16[512,512]{1,0:T(8,128)(2,1)} %medium.3.refs_0_), channel_id=1, source_target_pairs={{0,2},{1,3},{2,4},{3,5},{4,6},{5,7},{6,0},{7,1},{8,10},{9,11},{10,... | collective-permute-start | bytes 1572872 | tf_op jit(solution)/shard_map/ppermute | solution.py:296
  144.5 26.1 %collective-permute-start.4 = (bf16[512,512]{1,0:T(8,128)(2,1)}, bf16[512,512]{1,0:T(8,128)(2,1)S(1)}, u32[]{:S(2)}, u32[]{:S(2)}) collective-permute-start(bf16[512,512]{1,0:T(8,128)(2,1)} %medium.3.refs_0_), channel_id=1, source_target_pairs={{0,1},{1,0},{2,3},{3,2},{4,5},{5,4},{6,7},{7,6},{8,9},{9,8},{10,11... | collective-permute-start | bytes 1572872 | tf_op jit(solution)/shard_map/ppermute | solution.py:306
  145.4 25.3 %collective-permute-start.5 = (bf16[512,512]{1,0:T(8,128)(2,1)S(1)}, bf16[512,512]{1,0:T(8,128)(2,1)S(1)}, u32[]{:S(2)}, u32[]{:S(2)}) collective-permute-start(bf16[512,512]{1,0:T(8,128)(2,1)S(1)} %collective-permute-done.1.refs_1_), channel_id=1, source_target_pairs={{0,1},{1,0},{2,3},{3,2},{4,5},{5,4},{6,7},{7,6},{8,9},{9,8},{10,11... | collective-permute-start | bytes 1572872 | tf_op jit(solution)/shard_map/ppermute | solution.py:306
  179.2 26.8 %collective-permute-start.39 = (bf16[528,512]{1,0:T(8,128)(2,1)S(1)}, bf16[528,512]{1,0:T(8,128)(2,1)}, u32[]{:S(2)}, u32[]{:S(2)}) collective-permute-start(bf16[528,512]{1,0:T(8,128)(2,1)S(1)} %get-tuple-element.18.refs_0_), channel_id=1, source_target_pairs={{0,6},{1,7},{2,0},{3,1},{4,2},{5,3},{6,4},{7,5},{8,14},{9,15},{10,... | collective-permute-start | bytes 1622024 | tf_op jit(solution)/shard_map/ppermute | solution.py:310
  181.9 17.2 %collective-permute-start.30 = (bf16[256,512]{1,0:T(8,128)(2,1)S(1)}, bf16[256,512]{1,0:T(8,128)(2,1)S(1)}, u32[]{:S(2)}, u32[]{:S(2)}) collective-permute-start(bf16[256,512]{1,0:T(8,128)(2,1)S(1)} %slice.60), channel_id=1, source_target_pairs={{0,6},{1,7},{2,0},{3,1},{4,2},{5,3},{6,4},{7,5},{8,14},{9,15},{10,... | collective-permute-start | bytes 786440 | tf_op jit(solution)/shard_map/ppermute | solution.py:312
  185.7 20.8 %collective-permute-start.41 = (bf16[528,512]{1,0:T(8,128)(2,1)S(1)}, bf16[528,512]{1,0:T(8,128)(2,1)S(1)}, u32[]{:S(2)}, u32[]{:S(2)}) collective-permute-start(bf16[528,512]{1,0:T(8,128)(2,1)S(1)} %get-tuple-element.18.refs_0_), channel_id=1, source_target_pairs={{0,2},{1,3},{2,4},{3,5},{4,6},{5,7},{6,0},{7,1},{8,10},{9,11},{10,... | collective-permute-start | bytes 1622024 | tf_op jit(solution)/shard_map/ppermute | solution.py:311
  186.2 19.8 %collective-permute-start.32 = (bf16[272,512]{1,0:T(8,128)(2,1)S(1)}, bf16[272,512]{1,0:T(8,128)(2,1)S(1)}, u32[]{:S(2)}, u32[]{:S(2)}) collective-permute-start(bf16[272,512]{1,0:T(8,128)(2,1)S(1)} %slice.61), channel_id=1, source_target_pairs={{0,2},{1,3},{2,4},{3,5},{4,6},{5,7},{6,0},{7,1},{8,10},{9,11},{10,... | collective-permute-start | bytes 835592 | tf_op jit(solution)/shard_map/ppermute | solution.py:313
  187.3 20.2 %collective-permute-start.34 = (bf16[528,512]{1,0:T(8,128)(2,1)S(1)}, bf16[528,512]{1,0:T(8,128)(2,1)S(1)}, u32[]{:S(2)}, u32[]{:S(2)}) collective-permute-start(bf16[528,512]{1,0:T(8,128)(2,1)S(1)} %collective-permute-done.29.refs_1_), channel_id=1, source_target_pairs={{0,1},{1,0},{2,3},{3,2},{4,5},{5,4},{6,7},{7,6},{8,9},{9,8},{10,11... | collective-permute-start | bytes 1622024 | tf_op jit(solution)/shard_map/ppermute | solution.py:315
  206.5 22.7 %collective-permute-start.43 = (bf16[528,512]{1,0:T(8,128)(2,1)S(1)}, bf16[528,512]{1,0:T(8,128)(2,1)}, u32[]{:S(2)}, u32[]{:S(2)}) collective-permute-start(bf16[528,512]{1,0:T(8,128)(2,1)S(1)} %get-tuple-element.18.refs_0_), channel_id=1, source_target_pairs={{0,1},{1,0},{2,3},{3,2},{4,5},{5,4},{6,7},{7,6},{8,9},{9,8},{10,11... | collective-permute-start | bytes 1622024 | tf_op jit(solution)/shard_map/ppermute | solution.py:315
  207.5 25.6 %collective-permute-start.44 = (bf16[528,512]{1,0:T(8,128)(2,1)}, bf16[528,512]{1,0:T(8,128)(2,1)}, u32[]{:S(2)}, u32[]{:S(2)}) collective-permute-start(bf16[528,512]{1,0:T(8,128)(2,1)} %collective-permute-done.39.refs_1_), channel_id=1, source_target_pairs={{0,1},{1,0},{2,3},{3,2},{4,5},{5,4},{6,7},{7,6},{8,9},{9,8},{10,11... | collective-permute-start | bytes 1622024 | tf_op jit(solution)/shard_map/ppermute | solution.py:315
  207.7 25.4 %collective-permute-start.47 = (bf16[528,512]{1,0:T(8,128)(2,1)S(1)}, bf16[528,512]{1,0:T(8,128)(2,1)}, u32[]{:S(2)}, u32[]{:S(2)}) collective-permute-start(bf16[528,512]{1,0:T(8,128)(2,1)S(1)} %collective-permute-done.41.refs_4_), channel_id=1, source_target_pairs={{0,1},{1,0},{2,3},{3,2},{4,5},{5,4},{6,7},{7,6},{8,9},{9,8},{10,11... | collective-permute-start | bytes 1622024 | tf_op jit(solution)/shard_map/ppermute | solution.py:315
  256.4 33.2 %collective-permute-start.54 = (bf16[16,512]{1,0:T(8,128)(2,1)S(1)}, bf16[16,512]{1,0:T(8,128)(2,1)S(1)}, u32[]{:S(2)}, u32[]{:S(2)}) collective-permute-start(bf16[16,512]{1,0:T(8,128)(2,1)S(1)} %fusion.15), channel_id=1, source_target_pairs={{0,32},{8,40},{16,48},{24,56},{32,64},{40,72},{48,80},{56,88},{64,... | collective-permute-start | bytes 49160 | tf_op jit(solution)/shard_map/ppermute | solution.py:296
  269.6 20.0 %collective-permute-start.53 = (bf16[16,512]{1,0:T(8,128)(2,1)S(1)}, bf16[16,512]{1,0:T(8,128)(2,1)S(1)}, u32[]{:S(2)}, u32[]{:S(2)}) collective-permute-start(bf16[16,512]{1,0:T(8,128)(2,1)S(1)} %fusion.15), channel_id=1, source_target_pairs={{0,64},{8,72},{16,80},{24,88},{32,96},{40,104},{48,112},{56,120},{... | collective-permute-start | bytes 49160 | tf_op jit(solution)/shard_map/ppermute | solution.py:296
  269.6 20.0 %collective-permute-start.52 = (bf16[16,512]{1,0:T(8,128)(2,1)S(1)}, bf16[16,512]{1,0:T(8,128)(2,1)S(1)}, u32[]{:S(2)}, u32[]{:S(2)}) collective-permute-start(bf16[16,512]{1,0:T(8,128)(2,1)S(1)} %fusion.15), channel_id=1, source_target_pairs={{0,96},{8,104},{16,112},{24,120},{32,0},{40,8},{48,16},{56,24},{64... | collective-permute-start | bytes 49160 | tf_op jit(solution)/shard_map/ppermute | solution.py:296
  (89 other events, 1025.9 us)
Sparse Core Ops, SparseCore 0:
  27.2 99.8 all-gather.6
  129.2 53.2 all-gather.4
